TPU v7x, 256 devices: a whole 4x4x8 slice. The times are simulated.
256 devices in a mesh: rep: 16 (over x, z_lo), tp: 16 (over z_hi, y, core).
Axes of the slice: x: 4, y: 4, z: 8 (z_hi: 2, z_lo: 4; z = z_hi * 4 + z_lo), core: 2. Of those that a mesh axis runs over, the one named last changes fastest.
Arguments:
- hidden: bfloat16 [16384, 4096], P('rep'), may hold values from -6 to 6
- norm_gain: bfloat16 [4096], replicated, may hold values from 0.099609375 to 1.8984375
- w_query: bfloat16 [4096, 4096], P('rep', 'tp'), may hold values from -0.09375 to 0.09375
- w_keyval: bfloat16 [4096, 1024], P('rep', 'tp'), may hold values from -0.09375 to 0.09375
- w_output: bfloat16 [4096, 4096], P('tp', 'rep'), may hold values from -0.09375 to 0.09375
- cache: bfloat16 [32768, 1024], P('rep'), may hold values from -190 to 190
- lengths: int32 [16, 4], P('rep'), may hold values from 1 to 640, 1024 in all within a row
- prefix: int32 [64], P('rep'), may hold values from 1 to 512, 16384 in all
- out_gain: bfloat16 [4096], replicated, may hold values from 0.099609375 to 1.8984375
Outputs:
- resid: bfloat16 [16384, 4096], P('rep', 'tp')
- normed: bfloat16 [16384, 4096], P('rep', 'tp')
Inputs may be any that keep to these rules, and one draw needn't show every extreme that they name: `lengths`: each row sums to 1024, and some request has 640 new tokens. All prefixes sum to 16384, and some request has a prefix of 512.
All inputs are finite; a program needn't handle non-finite values. No bound on the sum of `prefix` on one device may be relied on, other than what follows from the above.
Results may differ from a plain program's by a relative error of at most 0.0095.
Values may be sent and summed in bfloat16 or wider, within the bound.
A program may use at most 128 MiB of HBM per device.

v0:
```python
import jax
import jax.numpy as jnp
from jax import lax
from jax.sharding import PartitionSpec as P

H = 32
KV = 4
HD = 128
REQ_REP = 4
PREF_MAX = 512
MOST_LEN = 640


norm_eps = 1e-05
rope_base = 5000000.0
masked_score = -1e30


def rms_scale(values, weights):
    meansq = jnp.mean(values * values, axis=-1, keepdims=True)
    return values * lax.rsqrt(meansq + norm_eps) * weights


def rotate(values, positions):
    half_dim = values.shape[-1] // 2
    freqs = rope_base ** (-(jnp.arange(half_dim, dtype=jnp.float32) * 2.0 / values.shape[-1]))
    angles = positions.astype(jnp.float32)[:, None] * freqs[None, :]
    cosine = jnp.cos(angles)[:, None, :]
    sine = jnp.sin(angles)[:, None, :]
    first = values[..., :half_dim]
    second = values[..., half_dim:]
    return jnp.concatenate(
        [first * cosine - second * sine, second * cosine + first * sine], axis=-1
    )


def request_layout(lens, prefs, count):
    token_ids = jnp.arange(count, dtype=jnp.int32)
    ends = jnp.cumsum(lens)
    starts = ends - lens
    segment = jnp.sum((token_ids[:, None] >= ends[None, :]).astype(jnp.int32), axis=1)
    onehot = segment[:, None] == jnp.arange(lens.shape[0], dtype=jnp.int32)[None, :]
    offset = token_ids - jnp.sum(jnp.where(onehot, starts[None, :], 0), axis=1)
    position = offset + jnp.sum(jnp.where(onehot, prefs[None, :], 0), axis=1)
    return (token_ids, segment, position, starts)


def body(hidden, norm_gain, w_query, w_keyval, w_output, cache, lengths, prefix, out_gain):
    tp_count = lax.axis_size("tp")
    tp_index = lax.axis_index("tp")
    rows = hidden.shape[0]
    normed_in = rms_scale(hidden.astype(jnp.float32), norm_gain.astype(jnp.float32)).astype(
        jnp.bfloat16
    )
    query_raw = jnp.dot(
        normed_in,
        lax.all_gather(w_query, "rep", axis=0, tiled=True),
        preferred_element_type=jnp.float32,
    )
    fresh_part = jnp.dot(
        normed_in,
        lax.all_gather(w_keyval, "rep", axis=0, tiled=True),
        preferred_element_type=jnp.float32,
    )
    fresh_all = lax.all_gather(fresh_part.astype(jnp.bfloat16), "tp", axis=1, tiled=True)
    heads_here = w_query.shape[1] // HD
    kv_head = tp_index * heads_here // (H // KV)
    kv_count = fresh_all.shape[1] // (2 * HD)
    fresh_head = lax.dynamic_slice_in_dim(fresh_all.reshape(rows, 2 * HD, kv_count), kv_head, 1, 2)
    fresh_head = fresh_head.reshape(rows, 2 * HD)
    lens = lengths.reshape(-1)
    token_ids, segment, position, starts = request_layout(lens, prefix, rows)
    queries = rotate(query_raw.reshape(rows, heads_here, HD), position).astype(jnp.bfloat16)
    queries = queries.transpose(1, 0, 2)
    new_keys = rotate(fresh_head[:, :HD].astype(jnp.float32).reshape(rows, 1, HD), position)
    new_keys = new_keys.reshape(rows, HD).astype(jnp.bfloat16)
    new_vals = fresh_head[:, HD:]
    stored = lax.dynamic_slice_in_dim(cache, kv_head * 2 * HD, 2 * HD, 1)
    scale = HD ** (-0.5)
    slot_range = jnp.arange(PREF_MAX, dtype=jnp.int32)
    attended_all = jnp.zeros((heads_here, rows, HD), jnp.float32)
    for request in range(REQ_REP):
        first = jnp.minimum(starts[request], rows - MOST_LEN)
        query_window = lax.dynamic_slice_in_dim(queries, first, MOST_LEN, 1)
        key_window = lax.dynamic_slice_in_dim(new_keys, first, MOST_LEN, 0)
        value_window = lax.dynamic_slice_in_dim(new_vals, first, MOST_LEN, 0)
        segment_window = lax.dynamic_slice_in_dim(segment, first, MOST_LEN, 0)
        ids_window = lax.dynamic_slice_in_dim(token_ids, first, MOST_LEN, 0)
        entries = stored[request * PREF_MAX : (request + 1) * PREF_MAX]
        row_ok = segment_window == request
        cache_ok = row_ok[:, None] & (slot_range < prefix[request])[None, :]
        own_ok = row_ok[:, None] & row_ok[None, :] & (ids_window[None, :] <= ids_window[:, None])
        allowed = jnp.concatenate([cache_ok, own_ok], axis=1)
        key_all = jnp.concatenate([entries[:, :HD], key_window], axis=0)
        value_all = jnp.concatenate([entries[:, HD:], value_window], axis=0)
        scores = (
            jnp.einsum("htd,sd->hts", query_window, key_all, preferred_element_type=jnp.float32)
            * scale
        )
        scores = jnp.where(allowed[None], scores, masked_score)
        peak = jnp.max(scores, axis=-1, keepdims=True)
        expo = jnp.where(allowed[None], jnp.exp(scores - peak), 0.0)
        total = jnp.sum(expo, axis=-1)
        summed = jnp.einsum(
            "hts,sd->htd", expo.astype(jnp.bfloat16), value_all, preferred_element_type=jnp.float32
        )
        result = summed / jnp.where(row_ok[None, :], total, 1.0)[..., None]
        current = lax.dynamic_slice_in_dim(attended_all, first, MOST_LEN, 1)
        merged = jnp.where(row_ok[None, :, None], result, current)
        attended_all = lax.dynamic_update_slice_in_dim(attended_all, merged, first, 1)
    attended = attended_all.astype(jnp.bfloat16)
    attended = attended.transpose(1, 0, 2).reshape(rows, heads_here * HD)
    partial_out = jnp.dot(
        attended,
        lax.all_gather(w_output, "rep", axis=1, tiled=True),
        preferred_element_type=jnp.float32,
    )
    width = hidden.shape[1] // tp_count
    summed_all = lax.psum(partial_out.astype(jnp.bfloat16), "tp").astype(jnp.float32)
    resid_full = (hidden.astype(jnp.float32) + summed_all).astype(jnp.bfloat16)
    normed_full = rms_scale(resid_full.astype(jnp.float32), out_gain.astype(jnp.float32)).astype(
        jnp.bfloat16
    )
    resid = lax.dynamic_slice_in_dim(resid_full, tp_index * width, width, 1)
    normed = lax.dynamic_slice_in_dim(normed_full, tp_index * width, width, 1)
    return (resid, normed)


def solution(mesh):
    placed = (
        P("rep", None),
        P(),
        P("rep", "tp"),
        P("rep", "tp"),
        P("tp", "rep"),
        P("rep", None),
        P("rep", None),
        P("rep"),
        P(),
    )
    return jax.shard_map(
        body,
        mesh=mesh,
        in_specs=placed,
        out_specs=(P("rep", "tp"), P("rep", "tp")),
        check_vma=False,
    )
```

profile of v0, /device:TPU:1, one launch (start us, length us, event | category | flops | bytes accessed | tf_op | source)
XLA Modules:
  0.0 518.0 jit_solution(5282601694610375687)
XLA Ops:
  7.2 0.7 all-gather.4.cloned.1.call-update
  8.0 0.9 convert_element_type.63
  8.8 5.2 %fusion.4 = f32[1024]{0:T(1024)S(1)} fusion(bf16[1024,4096]{1,0:T(8,128)(2,1)} %param.9), kind=kLoop, calls=%fused_computation.7 | loop fusion | flops 12581888 | bytes 8392704 | tf_op jit(solution)/shard_map/reduce_sum | solution.py:20
  14.0 46.8 %all_gather.13 = bf16[4096,64]{0,1:T(8,128)(2,1)S(1)} all-gather(bf16[256,64]{0,1:T(8,128)(2,1)S(1)} %copy-done.15), channel_id=1, replica_groups=mesh['rep'=16,'tp'=16] {'rep'}, dimensions={0}, use_global_device_ids=true | all-gather | bytes 557056 | tf_op jit(solution)/shard_map/all_gather | solution.py:62
  60.8 3.5 fusion.40
  64.4 0.7 all-gather.8.cloned.1.call-update
  65.1 0.3 all-reduce.2.cloned.1.call-start
  65.6 0.6 fusion.163
  68.9 0.7 fusion.162
  69.6 0.6 iota_compare_fusion.4
  70.2 0.7 iota_compare_fusion.5
  70.9 2.2 fusion.159
  73.1 0.8 copy.52
  73.9 0.8 copy.54
  75.2 0.7 iota_compare_fusion.2
  75.8 0.6 iota_compare_fusion.3
  76.4 0.8 copy.56
  77.2 0.8 copy.58
  77.9 1.0 compare_and_fusion.2
  78.9 0.4 broadcast_and_fusion.2
  79.3 0.9 pad_add_fusion
  80.2 3.0 multiply_cosine_fusion
  83.2 0.9 pad_add_fusion.1
  84.2 1.0 compare_and_fusion
  85.1 0.4 broadcast_and_fusion
  85.5 1.0 pad_add_fusion.2
  86.5 0.9 pad_add_fusion.3
  87.4 7.5 %all-gather.4.cloned.1.call-done = bf16[4096,256]{1,0:T(8,128)(2,1)} async-done(((bf16[256,256]{1,0:T(8,128)(2,1)}), bf16[4096,256]{1,0:T(8,128)(2,1)}) %all-gather.4.cloned.1.call-update) | async-done | bytes 2097168 | tf_op jit(solution)/shard_map/all_gather | solution.py:57
  94.9 6.2 %fusion.38 = f32[1024,256]{0,1:T(8,128)S(1)} fusion(bf16[4096,256]{1,0:T(8,128)(2,1)} %all-gather.4.cloned.1.call-done, bf16[1024,4096]{1,0:T(8,128)(2,1)} %param.9, f32[4096]{0:T(1024)S(1)} %convert_element_type.63, f32[1024]{0:T(1024)S(1)} %add_rsqrt_fusion.1), kind=kOutput, calls=%fused_computation.50 | convolution fusion | flops 2164260864 | bytes 11554816 | tf_op jit(solution)/shard_map/dot_general | solution.py:55
  101.2 1.3 copy.59
  102.6 1.3 copy.60
  103.9 63.0 %all-gather.6.cloned.1.call-done = bf16[1024,1024]{0,1:T(8,128)(2,1)} async-done(((bf16[1024,64]{0,1:T(8,128)(2,1)}), bf16[1024,1024]{0,1:T(8,128)(2,1)}) %all-gather.6.cloned.1.call-update) | async-done | bytes 2097168 | tf_op jit(solution)/shard_map/all_gather | solution.py:65
  166.9 2.7 reshape.274
  169.6 1.1 constant_dynamic-slice_fusion.6
  170.7 0.9 copy.61
  171.9 1.7 fusion.92
  173.6 0.9 constant_dynamic-slice_fusion.2
  174.5 1.8 add_convert_fusion
  176.4 0.5 fusion.93
  177.0 1.7 copy.64
  178.7 0.8 copy.53
  179.5 1.7 copy.65
  181.2 2.0 fusion.74
  183.2 4.0 fusion.12
  187.3 4.4 fusion.48
  191.8 4.4 dynamic_update_slice.12
  196.2 4.1 fusion.14
  200.3 4.6 fusion.54
  204.9 5.6 %dynamic_update_slice.13 = bf16[2,1024,128]{1,2,0:T(8,128)(2,1)S(1)} dynamic-update-slice(bf16[2,1024,128]{1,2,0:T(8,128)(2,1)S(1)} %dynamic_update_slice.12, bf16[2,640,128]{1,2,0:T(8,128)(2,1)S(1)} %fusion.54, s32[]{:T(128)} %constant.25.clone.1, s32[]{:T(128)S(6)} %select_n.134, s32[]{:T(128)} %constant.25.clone.1) | dynamic-update-slice | bytes 655364 | tf_op jit(solution)/shard_map/dynamic_update_slice | solution.py:110
  210.9 4.1 fusion.16
  215.0 4.4 fusion.60
  219.5 5.0 dynamic_update_slice.14
  224.9 4.1 fusion.18
  229.0 3.3 fusion.66
  232.4 3.3 dynamic_update_slice.15
  235.7 3.4 all-gather.8.cloned.1.call-done
  239.1 7.2 %convolution_convert_fusion = bf16[1024,4096]{1,0:T(8,128)(2,1)} fusion(bf16[1024,256]{0,1:T(8,128)(2,1)S(1)} %bitcast.115, bf16[256,4096]{1,0:T(8,128)(2,1)} %all-gather.8.cloned.1.call-done), kind=kOutput, calls=%fused_computation.12 | convolution fusion | flops 2151677952 | bytes 11010048 | tf_op jit(solution)/shard_map/dot_general | solution.py:113
  246.3 0.8 dynamic-slice.36
  247.1 238.6 %all-reduce.2.cloned.1.call-done = bf16[1024,4096]{1,0:T(8,128)(2,1)} async-done(((bf16[1024,4096]{1,0:T(8,128)(2,1)}), bf16[1024,4096]{1,0:T(8,128)(2,1)}) %all-reduce.2.cloned.1.call-update) | async-done | bytes 8388624 | tf_op jit(solution)/shard_map/psum | solution.py:119
  485.7 7.8 %multiply_reduce_fusion = (f32[1024]{0:T(1024)S(1)}, bf16[1024,4096]{1,0:T(8,128)(2,1)S(1)}) fusion(bf16[1024,4096]{1,0:T(8,128)(2,1)} %all-reduce.2.cloned.1.call-done, bf16[1024,4096]{1,0:T(8,128)(2,1)} %param.9), kind=kLoop, calls=%fused_computation.11 | loop fusion | flops 29359104 | bytes 25169920 | tf_op jit(solution)/shard_map/reduce_sum | solution.py:20
  493.5 3.2 copy-done
  496.8 0.9 constant_dynamic-slice_fusion.1
  497.6 11.4 %convert_element_type.75 = f32[1024,4096]{1,0:T(8,128)} convert(bf16[1024,4096]{1,0:T(8,128)(2,1)} %copy-done) | non-fusion elementwise | flops 4194304 | bytes 25165824 | tf_op jit(solution)/shard_map/convert_element_type | solution.py:121
  509.0 2.2 fusion.44
  (72 shorter events, 2.2 us)
Async XLA Ops:
  7.2 6.9 %copy-start.15 = (bf16[256,64]{0,1:T(8,128)(2,1)S(1)}, bf16[256,64]{0,1:T(8,128)(2,1)}, u32[]{:S(2)}) copy-start(bf16[256,64]{0,1:T(8,128)(2,1)} %param.12) | copy-start | bytes 98308
  7.2 87.7 %all-gather.4.cloned.1.call-start = ((), (), s32[]{:S(2)}) async-start(), calls=%async_computation | async-start | bytes 2228224 | tf_op jit(solution)/shard_map/all_gather | solution.py:57
  7.9 159.0 %all-gather.6.cloned.1.call-start = ((), (), s32[]{:S(2)}) async-start(), calls=%async_computation.1 | async-start | bytes 2228224 | tf_op jit(solution)/shard_map/all_gather | solution.py:65
  8.0 52.9 %copy-start.1 = (bf16[1024,4096]{1,0:T(8,128)(2,1)S(1)}, bf16[1024,4096]{1,0:T(8,128)(2,1)}, u32[]{:S(2)}) copy-start(bf16[1024,4096]{1,0:T(8,128)(2,1)} %param.9) | copy-start | bytes 25165828
  60.8 4.6 copy-start.17
  60.8 8.1 %copy-start.16 = (s32[4]{0:T(128)S(1)}, s32[4]{0:T(128)}, u32[]{:S(2)}) copy-start(s32[4]{0:T(128)} %param.16) | copy-start | bytes 52
  64.3 174.8 %all-gather.8.cloned.1.call-start = ((), (), s32[]{:S(2)}) async-start(), calls=%async_computation.2 | async-start | bytes 2228224 | tf_op jit(solution)/shard_map/all_gather | solution.py:115
  65.1 420.6 %all-reduce.2.cloned.1.call-start = ((), (), s32[]{:S(2)}) async-start(), calls=%async_computation.3 | async-start | bytes 16777216 | tf_op jit(solution)/shard_map/psum | solution.py:119
  170.7 3.8 copy-start.2
  171.9 11.4 %copy-start.6 = (pred[640,1152]{1,0:T(8,128)(4,1)S(1)}, pred[640,1152]{1,0:T(8,128)(4,1)}, u32[]{:S(2)}) copy-start(pred[640,1152]{1,0:T(8,128)(4,1)} %pad_add_fusion) | copy-start | bytes 2211844
  187.3 8.9 %copy-start.5 = (pred[640,1152]{1,0:T(8,128)(4,1)S(1)}, pred[640,1152]{1,0:T(8,128)(4,1)}, u32[]{:S(2)}) copy-start(pred[640,1152]{1,0:T(8,128)(4,1)} %pad_add_fusion.1) | copy-start | bytes 2211844
  187.3 8.9 %copy-start.9 = (bf16[2,640,128]{2,1,0:T(8,128)(2,1)S(1)}, bf16[2,640,128]{2,1,0:T(8,128)(2,1)}, u32[]{:S(2)}) copy-start(bf16[2,640,128]{2,1,0:T(8,128)(2,1)} %get-tuple-element.18) | copy-start | bytes 983044
  187.3 8.9 %copy-start.10 = (bf16[640,1,128]{2,0,1:T(8,128)(2,1)S(1)}, bf16[640,1,128]{2,0,1:T(8,128)(2,1)}, u32[]{:S(2)}) copy-start(bf16[640,1,128]{2,0,1:T(8,128)(2,1)} %copy.53) | copy-start | bytes 491524
  196.2 4.1 copy-start.11
  200.3 10.6 %copy-start.4 = (pred[640,1152]{1,0:T(8,128)(4,1)S(1)}, pred[640,1152]{1,0:T(8,128)(4,1)}, u32[]{:S(2)}) copy-start(pred[640,1152]{1,0:T(8,128)(4,1)} %pad_add_fusion.2) | copy-start | bytes 2211844
  200.3 10.6 %copy-start.8 = (bf16[2,640,128]{2,1,0:T(8,128)(2,1)S(1)}, bf16[2,640,128]{2,1,0:T(8,128)(2,1)}, u32[]{:S(2)}) copy-start(bf16[2,640,128]{2,1,0:T(8,128)(2,1)} %get-tuple-element.19) | copy-start | bytes 983044
  210.9 4.1 copy-start.13
  215.0 9.8 %copy-start.3 = (pred[640,1152]{1,0:T(8,128)(4,1)S(1)}, pred[640,1152]{1,0:T(8,128)(4,1)}, u32[]{:S(2)}) copy-start(pred[640,1152]{1,0:T(8,128)(4,1)} %pad_add_fusion.3) | copy-start | bytes 2211844
  215.0 9.8 %copy-start.7 = (bf16[2,640,128]{2,1,0:T(8,128)(2,1)S(1)}, bf16[2,640,128]{2,1,0:T(8,128)(2,1)}, u32[]{:S(2)}) copy-start(bf16[2,640,128]{2,1,0:T(8,128)(2,1)} %get-tuple-element.16) | copy-start | bytes 983044
  224.9 4.1 copy-start.12
  224.9 4.1 copy-start.14
  493.5 3.2 copy-start
Sparse Core Ops, SparseCore 0:
  9.8 85.0 all-gather.3
  97.6 69.2 all-gather.5
  168.6 70.4 all-gather.7
  246.4 239.2 all-reduce.1
where the time goes:
time: 523 us; the launch traced here: 518 us
  waiting for transfers between devices  314 us (60%)
  matrix products  50 us (10%)
  blocking collectives  46.8 us (9%)
  other arithmetic  46 us (9%)
  local copies, waits for them, and re-layouts  43.7 us (8%)
  between operations  17.2 us (3%)
    psum x1, waiting for transfers between devices, body(): lax.psum(partial_out.astype(jnp.bfloat16), 'tp').astype(jnp.float32)  239 us
    all_gather x1, waiting for transfers between devices, body(): lax.all_gather(fresh_part.astype(jnp.bfloat16), 'tp', axis=1, tiled=True)  63 us
    all_gather x1, blocking collectives, body(): lax.all_gather(w_keyval, 'rep', axis=0, tiled=True)  46.8 us
    dynamic_update_slice x4, local copies, waits for them, and re-layouts, body(): lax.dynamic_update_slice_in_dim(attended_all, merged, first, 1)  18.3 us
    dot_general x4, matrix products, body(): jnp.einsum('hts,sd->htd', expo.astype(jnp.bfloat16), value_all, preferred...  16.8 us
    sub x4, matrix products, body(): expo = jnp.where(allowed[None], jnp.exp(scores - peak), 0.0)  16.3 us
    reduce_sum x2, other arithmetic, rms_scale(): meansq = jnp.mean(values * values, axis=-1, keepdims=True)  13 us
    convert_element_type x1, other arithmetic, body(): resid_full.astype(jnp.float32)  11.4 us
  transfers between devices with their start and end apart: 4, of which 4 were waited for; matrix products, arithmetic and copies ran while one was open for 21% of the time, Pallas kernels for 0%

commit v1 on v0

v1 whole, which is shorter than its diff:
```python
import functools
import math

import jax
import jax.numpy as jnp
from jax import lax
from jax.experimental import pallas as pl
from jax.experimental.pallas import tpu as pltpu
from jax.sharding import PartitionSpec as P

H = 32
KV = 4
HD = 128
REQ_REP = 4
PREF_MAX = 512

norm_eps = 1e-05
rope_base = 5000000.0
TQ = 128
KB = 256
NEG_START = -1e30
NEG_MASK = -2e30


def rms_scale(values, weights):
    meansq = jnp.mean(values * values, axis=-1, keepdims=True)
    return values * lax.rsqrt(meansq + norm_eps) * weights


def rotate(values, positions):
    half_dim = values.shape[-1] // 2
    freqs = rope_base ** (-(jnp.arange(half_dim, dtype=jnp.float32) * 2.0 / values.shape[-1]))
    angles = positions.astype(jnp.float32)[:, None] * freqs[None, :]
    cosine = jnp.cos(angles)[:, None, :]
    sine = jnp.sin(angles)[:, None, :]
    first = values[..., :half_dim]
    second = values[..., half_dim:]
    return jnp.concatenate(
        [first * cosine - second * sine, second * cosine + first * sine], axis=-1
    )


def request_layout(lens, prefs, count):
    token_ids = jnp.arange(count, dtype=jnp.int32)
    ends = jnp.cumsum(lens)
    starts = ends - lens
    segment = jnp.sum((token_ids[:, None] >= ends[None, :]).astype(jnp.int32), axis=1)
    onehot = segment[:, None] == jnp.arange(lens.shape[0], dtype=jnp.int32)[None, :]
    offset = token_ids - jnp.sum(jnp.where(onehot, starts[None, :], 0), axis=1)
    position = offset + jnp.sum(jnp.where(onehot, prefs[None, :], 0), axis=1)
    return position, starts, ends


def attention_kernel(meta, q_ref, k_ref, v_ref, cache_ref, o_ref, stored, m_ref, l_ref, acc_ref, sems):
    kv_head = meta[12]
    column = pl.multiple_of(kv_head * 2 * HD, 2 * HD)
    copies = []
    for request in range(REQ_REP):
        rows = pl.ds(request * PREF_MAX, PREF_MAX)
        copies.append(
            pltpu.make_async_copy(
                cache_ref.at[rows, pl.ds(column, 2 * HD)], stored.at[rows, :], sems.at[request]
            )
        )
        copies[-1].start()
    factor = HD ** (-0.5) * math.log2(math.e)
    heads = q_ref.shape[1] // HD

    def step(q, key, value, mask):
        s = lax.dot_general(q, key, (((1,), (1,)), ((), ())), preferred_element_type=jnp.float32)
        if mask is not None:
            s = jnp.where(mask, s, NEG_MASK)
        old = m_ref[...]
        new = jnp.maximum(old, jnp.max(s, axis=1, keepdims=True))
        shrink = jnp.exp2((old - new) * factor)
        m_ref[...] = new
        p = jnp.exp2((s - new[:, :1]) * factor)
        folded = p[:, :HD]
        for part in range(1, KB // HD):
            folded = folded + p[:, part * HD : (part + 1) * HD]
        l_ref[...] = l_ref[...] * shrink + folded
        acc_ref[...] = acc_ref[...] * shrink + jnp.dot(
            p.astype(jnp.bfloat16), value, preferred_element_type=jnp.float32
        )

    shape = (heads * TQ, KB)
    lane = lax.broadcasted_iota(jnp.int32, shape, 1)
    row = lax.rem(lax.broadcasted_iota(jnp.int32, shape, 0), TQ)
    for request in range(REQ_REP):
        start, end, prefix = meta[request], meta[4 + request], meta[8 + request]
        base = request * PREF_MAX
        copies[request].wait()

        def tile_body(tile, _):
            first = pl.multiple_of(tile * TQ, TQ)
            rows = pl.ds(first, TQ)
            q = jnp.concatenate([q_ref[rows, h * HD : (h + 1) * HD] for h in range(heads)], axis=0)
            m_ref[...] = jnp.full_like(m_ref, NEG_START)
            l_ref[...] = jnp.zeros_like(l_ref)
            acc_ref[...] = jnp.zeros_like(acc_ref)

            def full_block(block, _):
                at = pl.ds(base + pl.multiple_of(block * KB, KB), KB)
                step(q, stored[at, :HD], stored[at, HD:], None)
                return 0

            whole = prefix // KB
            lax.fori_loop(0, whole, full_block, 0)

            @pl.when(whole * KB < prefix)
            def _():
                at = pl.ds(base + pl.multiple_of(whole * KB, KB), KB)
                step(q, stored[at, :HD], stored[at, HD:], lane + whole * KB < prefix)

            def own_block(block, _):
                at = pl.ds(pl.multiple_of(block * KB, KB), KB)
                key_id = lane + block * KB
                step(q, k_ref[at, :], v_ref[at, :], (key_id >= start) & (key_id <= row + first))
                return 0

            def clear_block(block, _):
                at = pl.ds(pl.multiple_of(block * KB, KB), KB)
                step(q, k_ref[at, :], v_ref[at, :], None)
                return 0

            low = start // KB
            high = first // KB
            lax.fori_loop(low, jnp.minimum(low + 1, high), own_block, 0)
            lax.fori_loop(low + 1, high, clear_block, 0)
            own_block(high, 0)
            total = jnp.sum(l_ref[...], axis=1, keepdims=True)
            result = (acc_ref[...] / total).astype(o_ref.dtype)
            tok = first + lax.broadcasted_iota(jnp.int32, (TQ, HD), 0)
            own = (tok >= start) & (tok < end)
            for h in range(heads):
                at = slice(h * HD, (h + 1) * HD)
                o_ref[rows, at] = jnp.where(
                    own, result[h * TQ : (h + 1) * TQ].astype(jnp.float32), o_ref[rows, at].astype(jnp.float32)
                ).astype(o_ref.dtype)
            return 0

        lax.fori_loop(start // TQ, (end - 1) // TQ + 1, tile_body, 0)


def attend(meta, q, k, v, cache):
    rows, width = q.shape
    heads = width // HD
    return pl.pallas_call(
        attention_kernel,
        out_shape=jax.ShapeDtypeStruct((rows, width), jnp.bfloat16),
        in_specs=[
            pl.BlockSpec(memory_space=pltpu.SMEM),
            pl.BlockSpec(memory_space=pltpu.VMEM),
            pl.BlockSpec(memory_space=pltpu.VMEM),
            pl.BlockSpec(memory_space=pltpu.VMEM),
            pl.BlockSpec(memory_space=pl.ANY),
        ],
        out_specs=pl.BlockSpec(memory_space=pltpu.VMEM),
        scratch_shapes=[
            pltpu.VMEM((REQ_REP * PREF_MAX, 2 * HD), jnp.bfloat16),
            pltpu.VMEM((heads * TQ, HD), jnp.float32),
            pltpu.VMEM((heads * TQ, HD), jnp.float32),
            pltpu.VMEM((heads * TQ, HD), jnp.float32),
            pltpu.SemaphoreType.DMA((REQ_REP,)),
        ],
        cost_estimate=pl.CostEstimate(flops=2 * 10**9, bytes_accessed=3 * 2**20, transcendentals=2 * 10**6),
        name="attention",
    )(meta, q, k, v, cache)


def body(hidden, norm_gain, w_query, w_keyval, w_output, cache, lengths, prefix, out_gain):
    tp_count = lax.axis_size("tp")
    rep_count = lax.axis_size("rep")
    tp_index = lax.axis_index("tp")
    rows = hidden.shape[0]
    swapped = lax.ppermute(
        w_output,
        ("rep", "tp"),
        [(a * tp_count + b, b * tp_count + a) for a in range(rep_count) for b in range(tp_count)],
    )
    normed_in = rms_scale(hidden.astype(jnp.float32), norm_gain.astype(jnp.float32)).astype(
        jnp.bfloat16
    )
    query_raw = jnp.dot(
        normed_in,
        lax.all_gather(w_query, "rep", axis=0, tiled=True),
        preferred_element_type=jnp.float32,
    )
    fresh_part = jnp.dot(
        normed_in,
        lax.all_gather(w_keyval, "rep", axis=0, tiled=True),
        preferred_element_type=jnp.float32,
    )
    fresh_all = lax.all_gather(fresh_part.astype(jnp.bfloat16), "tp", axis=1, tiled=True)
    heads_here = w_query.shape[1] // HD
    kv_head = tp_index * heads_here // (H // KV)
    kv_count = fresh_all.shape[1] // (2 * HD)
    fresh_head = lax.dynamic_slice_in_dim(fresh_all.reshape(rows, 2 * HD, kv_count), kv_head, 1, 2)
    fresh_head = fresh_head.reshape(rows, 2 * HD)
    position, starts, ends = request_layout(lengths.reshape(-1), prefix, rows)
    queries = rotate(query_raw.reshape(rows, heads_here, HD), position).astype(jnp.bfloat16)
    queries = queries.reshape(rows, heads_here * HD)
    new_keys = rotate(fresh_head[:, :HD].astype(jnp.float32).reshape(rows, 1, HD), position)
    new_keys = new_keys.reshape(rows, HD).astype(jnp.bfloat16)
    new_vals = fresh_head[:, HD:]
    meta = jnp.concatenate([starts, ends, prefix, kv_head.reshape(1)]).astype(jnp.int32)
    attended = attend(meta, queries, new_keys, new_vals, cache)
    w_columns = lax.all_gather(swapped, "rep", axis=0, tiled=True)
    attended_all = lax.all_gather(attended, "tp", axis=1, tiled=True)
    width = hidden.shape[1] // tp_count
    proj = jnp.dot(attended_all, w_columns, preferred_element_type=jnp.float32)
    mine = lax.dynamic_slice_in_dim(hidden, tp_index * width, width, 1)
    gain = lax.dynamic_slice_in_dim(out_gain, tp_index * width, width, 0)
    resid = (mine.astype(jnp.float32) + proj).astype(jnp.bfloat16)
    wide = resid.astype(jnp.float32)
    meansq = lax.psum(jnp.sum(wide * wide, axis=-1, keepdims=True), "tp") / hidden.shape[1]
    normed = (wide * lax.rsqrt(meansq + norm_eps) * gain.astype(jnp.float32)).astype(jnp.bfloat16)
    return (resid, normed)


def solution(mesh):
    placed = (
        P("rep", None),
        P(),
        P("rep", "tp"),
        P("rep", "tp"),
        P("tp", "rep"),
        P("rep", None),
        P("rep", None),
        P("rep"),
        P(),
    )
    return jax.shard_map(
        body,
        mesh=mesh,
        in_specs=placed,
        out_specs=(P("rep", "tp"), P("rep", "tp")),
        check_vma=False,
    )
```

time: 523 us -> 474 us (0.906)
  blocking collectives: 46.8 us -> 84.4 us
  matrix products: 50 us -> 16.1 us
  local copies, waits for them, and re-layouts: 43.7 us -> 11.9 us
  other arithmetic: 46 us -> 18.6 us
  Pallas kernels: 0 us -> 20.4 us
  waiting for transfers between devices: 314 us -> 302 us
  starting transfers between devices: 0.45 us -> 6.29 us
    psum x1 -> x0, waiting for transfers between devices: 239 us -> none  [body(): lax.psum(partial_out.astype(jnp.bfloat16), 'tp').astype(jnp.float32)]
    all_gather x1 -> x2, waiting for transfers between devices: 3.43 us -> 174 us  [the longest x1 125 us: body(): attended_all = lax.all_gather(attended, 'tp', axis=1, tiled=True)]
    all_gather x1, waiting for transfers between devices: 7.51 us -> 69.6 us  [body(): lax.all_gather(w_query, 'rep', axis=0, tiled=True)]
    psum x0 -> x1, blocking collectives: none -> 42.4 us  [body(): lax.psum(jnp.sum(wide * wide, axis=-1, keepdims=True), 'tp')]
    pallas_call x0 -> x1, Pallas kernels: none -> 20.4 us  [attend(): pl.pallas_call(attention_kernel, out_shape=jax.ShapeDtypeStruct((rows, wi...]
    dynamic_update_slice x4 -> x0, local copies, waits for them, and re-layouts: 18.3 us -> none  [body(): lax.dynamic_update_slice_in_dim(attended_all, merged, first, 1)]
    dot_general x5 -> x1, matrix products: 24 us -> 6.39 us  [body(): proj = jnp.dot(attended_all, w_columns, preferred_element_type=jnp.float32)]
    sub x4 -> x0, matrix products: 16.3 us -> none  [body(): expo = jnp.where(allowed[None], jnp.exp(scores - peak), 0.0)]
  transfers between devices with their start and end apart: 4 -> 5, of which waited for: 4 -> 5; matrix products, arithmetic and copies ran while one was open for 21% -> 6% of each run, Pallas kernels for 0% -> 4%
where the time goes in v1:
time: 474 us
  waiting for transfers between devices  302 us (64%)
  blocking collectives  84.4 us (18%)
  Pallas kernels  20.4 us (4%)
  other arithmetic  18.6 us (4%)
  matrix products  16.1 us (3%)
  between operations  14 us (3%)
  local copies, waits for them, and re-layouts  11.9 us (3%)
  starting transfers between devices  6.29 us (1%)
    all_gather x1, waiting for transfers between devices, body(): attended_all = lax.all_gather(attended, 'tp', axis=1, tiled=True)  125 us
    all_gather x1, waiting for transfers between devices, body(): lax.all_gather(w_query, 'rep', axis=0, tiled=True)  69.6 us
    all_gather x1, waiting for transfers between devices, body(): lax.all_gather(fresh_part.astype(jnp.bfloat16), 'tp', axis=1, tiled=True)  54.1 us
    all_gather x1, waiting for transfers between devices, body(): w_columns = lax.all_gather(swapped, 'rep', axis=0, tiled=True)  49.6 us
    psum x1, blocking collectives, body(): lax.psum(jnp.sum(wide * wide, axis=-1, keepdims=True), 'tp')  42.4 us
    all_gather x1, blocking collectives, body(): lax.all_gather(w_keyval, 'rep', axis=0, tiled=True)  42 us
    pallas_call x1, Pallas kernels, attend(): pl.pallas_call(attention_kernel, out_shape=jax.ShapeDtypeStruct((rows, wi...  20.4 us
  transfers between devices with their start and end apart: 5, of which 5 were waited for; matrix products, arithmetic and copies ran while one was open for 6% of the time, Pallas kernels for 4%

profile of v1, /device:TPU:1, one launch (start us, length us, event | category | flops | bytes accessed | tf_op | source)
XLA Modules:
  0.0 473.7 jit_solution(11796663754386901824)
XLA Ops:
  7.2 0.0 copy-start.3
  7.2 0.0 all-gather.7.cloned.1.call-start
  7.2 0.0 copy-start
  7.2 0.9 convert_element_type.49
  8.1 5.2 %fusion = f32[1024]{0:T(1024)S(1)} fusion(bf16[1024,4096]{1,0:T(8,128)(2,1)} %param.9), kind=kLoop, calls=%fused_computation.2 | loop fusion | flops 12581888 | bytes 8392704 | tf_op jit(solution)/shard_map/reduce_sum | solution.py:26
  13.3 0.0 copy-done.3
  13.3 0.0 copy-start.5
  13.3 42.0 %all_gather.16 = bf16[4096,64]{0,1:T(8,128)(2,1)S(1)} all-gather(bf16[256,64]{0,1:T(8,128)(2,1)S(1)} %copy-done.3), channel_id=1, replica_groups=mesh['rep'=16,'tp'=16] {'rep'}, dimensions={0}, use_global_device_ids=true | all-gather | bytes 557056 | tf_op jit(solution)/shard_map/all_gather | solution.py:191
  55.4 0.0 copy-done
  55.4 0.0 copy-start.6
  55.4 0.0 copy-start.4
  55.4 3.5 fusion.8
  58.9 0.0 all-gather.7.cloned.1.call-update
  58.9 0.0 all-gather.5.cloned.1.call-start
  58.9 0.7 all-gather.5.cloned.1.call-update
  59.6 0.0 all-gather.11.cloned.1.call-start
  59.7 0.0 copy-done.5
  59.7 5.9 %collective-permute-start = (bf16[256,256]{1,0:T(8,128)(2,1)S(1)}, bf16[256,256]{1,0:T(8,128)(2,1)S(1)}, u32[]{:S(2)}, u32[]{:S(2)}) collective-permute-start(bf16[256,256]{1,0:T(8,128)(2,1)S(1)} %copy-done.5), channel_id=1, source_target_pairs={{0,0},{1,16},{2,32},{3,48},{4,64},{5,80},{6,96},{7,112},{8,128},{9... | collective-permute-start | bytes 393224 | tf_op jit(solution)/shard_map/ppermute | solution.py:176
  65.6 3.3 collective-permute-done
  68.9 0.0 copy-start.2
  68.9 0.7 copy-done.2
  69.6 0.0 all-gather.11.cloned.1.call-update
  69.6 0.2 all-gather.9.cloned.1.call-start
  69.9 0.0 copy-done.6
  69.9 0.2 reduce-window.4
  70.1 0.0 copy-done.4
  70.1 0.6 pad_add_fusion.meta
  70.6 0.1 convert_reduce_fusion
  70.7 0.1 select_reduce_fusion.1
  70.8 3.1 multiply_cosine_fusion.1
  73.9 54.1 %all-gather.7.cloned.1.call-done = bf16[1024,1024]{0,1:T(8,128)(2,1)} async-done(((bf16[1024,64]{0,1:T(8,128)(2,1)}), bf16[1024,1024]{0,1:T(8,128)(2,1)}) %all-gather.7.cloned.1.call-update) | async-done | bytes 2097168 | tf_op jit(solution)/shard_map/all_gather | solution.py:194
  128.0 2.7 reshape.169
  130.7 1.1 constant_dynamic-slice_fusion
  131.8 2.0 copy.39
  133.8 69.6 %all-gather.5.cloned.1.call-done = bf16[4096,256]{1,0:T(8,128)(2,1)} async-done(((bf16[256,256]{1,0:T(8,128)(2,1)}), bf16[4096,256]{1,0:T(8,128)(2,1)}) %all-gather.5.cloned.1.call-update) | async-done | bytes 2097168 | tf_op jit(solution)/shard_map/all_gather | solution.py:186
  203.4 6.2 %fusion.5 = f32[1024,256]{0,1:T(8,128)S(1)} fusion(bf16[4096,256]{1,0:T(8,128)(2,1)} %all-gather.5.cloned.1.call-done, bf16[1024,4096]{1,0:T(8,128)(2,1)} %param.9, f32[4096]{0:T(1024)S(1)} %convert_element_type.49, f32[1024]{0:T(1024)S(1)} %add_rsqrt_fusion.1), kind=kOutput, calls=%fused_computation.6 | convolution fusion | flops 2164260864 | bytes 11554816 | tf_op jit(solution)/shard_map/dot_general | solution.py:184
  209.6 0.0 copy-start.1
  209.6 0.1 fusion.24
  209.7 0.6 copy.37
  210.3 0.6 copy.38
  210.9 2.2 subtract_convert_fusion
  213.0 1.4 pad_maximum_fusion
  214.5 0.9 copy.42
  215.4 0.0 copy-done.1
  215.4 0.8 fusion.25
  216.1 2.4 fusion.19
  218.5 0.8 maximum_bitcast_fusion.k_ref
  219.4 20.4 %attention.1 = bf16[1024,256]{1,0:T(8,128)(2,1)} custom-call(s32[13]{0:T(128)} %pad_add_fusion.meta, bf16[1024,256]{1,0:T(8,128)(2,1)} %bitcast.36, bf16[1024,128]{1,0:T(8,128)(2,1)} %maximum_bitcast_fusion.k_ref, bf16[1024,128]{1,0:T(8,128)(2,1)} %get-tuple-element.18.v_ref, bf16[2048,1024]{1,0:T(8,128)(2,1)} %cache_ref.1), custom_call_target="tpu_custom_call" | custom-call | flops 2000000000 | bytes 3145728 | tf_op jit(solution)/shard_map/attention/pallas_call | solution.py:148
  239.8 0.0 all-gather.9.cloned.1.call-update
  239.8 1.1 constant_dynamic-slice_fusion.1
  240.9 0.2 copy.36
  241.1 0.8 dynamic-slice_convert_fusion
  241.9 49.6 %all-gather.11.cloned.1.call-done = bf16[4096,256]{1,0:T(8,128)(2,1)} async-done(((bf16[256,256]{1,0:T(8,128)(2,1)}), bf16[4096,256]{1,0:T(8,128)(2,1)}) %all-gather.11.cloned.1.call-update) | async-done | bytes 2097168 | tf_op jit(solution)/shard_map/all_gather | solution.py:208
  291.5 124.7 %all-gather.9.cloned.1.call-done = bf16[1024,4096]{1,0:T(8,128)(2,1)} async-done(((bf16[1024,256]{1,0:T(8,128)(2,1)}), bf16[1024,4096]{1,0:T(8,128)(2,1)}) %all-gather.9.cloned.1.call-update) | async-done | bytes 8388624 | tf_op jit(solution)/shard_map/all_gather | solution.py:209
  416.2 6.4 %fusion.11 = (f32[1024]{0:T(1024)S(1)}, bf16[1024,256]{0,1:T(8,128)(2,1)S(1)}) fusion(bf16[1024,4096]{1,0:T(8,128)(2,1)} %all-gather.9.cloned.1.call-done, bf16[4096,256]{1,0:T(8,128)(2,1)} %all-gather.11.cloned.1.call-done, bf16[1024,256]{0,1:T(8,128)(2,1)S(1)} %copy.36), kind=kOutput, calls=%fused_computation.12 | convolution fusion | flops 2149055488 | bytes 11538432 | tf_op jit(solution)/shard_map/dot_general | solution.py:211
  422.6 42.4 %psum.7 = f32[1024,1]{0,1:T(1,128)S(1)} all-reduce(f32[1024,1]{0,1:T(1,128)S(1)} %bitcast.38), channel_id=1, replica_groups=mesh['rep'=16,'tp'=16] {'tp'}, use_global_device_ids=true, to_apply=%region_6.7 | all-reduce | flops 1024 | bytes 8192 | tf_op jit(solution)/shard_map/psum | solution.py:216
  465.0 1.0 copy.34
  466.0 0.2 fusion.13
  466.2 1.0 copy.35
  (6 shorter events, 0.1 us)
Async XLA Ops:
  7.2 6.1 %copy-start.3 = (bf16[256,64]{0,1:T(8,128)(2,1)S(1)}, bf16[256,64]{0,1:T(8,128)(2,1)}, u32[]{:S(2)}) copy-start(bf16[256,64]{0,1:T(8,128)(2,1)} %param.12) | copy-start | bytes 98308
  7.2 120.8 %all-gather.7.cloned.1.call-start = ((), (), s32[]{:S(2)}) async-start(), calls=%async_computation.1 | async-start | bytes 2228224 | tf_op jit(solution)/shard_map/all_gather | solution.py:194
  7.2 48.2 %copy-start = (bf16[1024,4096]{1,0:T(8,128)(2,1)S(1)}, bf16[1024,4096]{1,0:T(8,128)(2,1)}, u32[]{:S(2)}) copy-start(bf16[1024,4096]{1,0:T(8,128)(2,1)} %param.9) | copy-start | bytes 25165828
  13.3 46.4 %copy-start.5 = (bf16[256,256]{1,0:T(8,128)(2,1)S(1)}, bf16[256,256]{1,0:T(8,128)(2,1)}, u32[]{:S(2)}) copy-start(bf16[256,256]{1,0:T(8,128)(2,1)} %param.13) | copy-start | bytes 393220
  55.4 14.5 %copy-start.6 = (s32[1,4]{1,0:T(1,128)S(1)}, s32[1,4]{1,0:T(1,128)}, u32[]{:S(2)}) copy-start(s32[1,4]{1,0:T(1,128)} %param.15) | copy-start | bytes 52
  55.4 14.7 %copy-start.4 = (s32[4]{0:T(128)S(1)}, s32[4]{0:T(128)}, u32[]{:S(2)}) copy-start(s32[4]{0:T(128)} %param.16) | copy-start | bytes 52
  58.9 144.5 %all-gather.5.cloned.1.call-start = ((), (), s32[]{:S(2)}) async-start(), calls=%async_computation | async-start | bytes 2228224 | tf_op jit(solution)/shard_map/all_gather | solution.py:186
  59.6 231.9 %all-gather.11.cloned.1.call-start = ((), (), s32[]{:S(2)}) async-start(), calls=%async_computation.3 | async-start | bytes 2228224 | tf_op jit(solution)/shard_map/all_gather | solution.py:208
  59.7 9.2 %collective-permute-start = (bf16[256,256]{1,0:T(8,128)(2,1)S(1)}, bf16[256,256]{1,0:T(8,128)(2,1)S(1)}, u32[]{:S(2)}, u32[]{:S(2)}) collective-permute-start(bf16[256,256]{1,0:T(8,128)(2,1)S(1)} %copy-done.5), channel_id=1, source_target_pairs={{0,0},{1,16},{2,32},{3,48},{4,64},{5,80},{6,96},{7,112},{8,128},{9... | collective-permute-start | bytes 393224 | tf_op jit(solution)/shard_map/ppermute | solution.py:176
  68.9 0.7 copy-start.2
  69.6 346.6 %all-gather.9.cloned.1.call-start = ((), (), s32[]{:S(2)}) async-start(), calls=%async_computation.2 | async-start | bytes 8912896 | tf_op jit(solution)/shard_map/all_gather | solution.py:209
  209.6 5.7 %copy-start.1 = (bf16[1024,256,1]{1,0,2:T(8,128)(2,1)S(1)}, bf16[1024,256,1]{1,0,2:T(8,128)(2,1)}, u32[]{:S(2)}) copy-start(bf16[1024,256,1]{1,0,2:T(8,128)(2,1)} %copy.39) | copy-start | bytes 1572868
Sparse Core Ops, SparseCore 0:
  59.0 68.9 all-gather.6
  129.8 73.5 all-gather.4
  205.2 86.3 all-gather.10
  294.5 121.6 all-gather.8

commit v2 on v1

v2 whole, which is shorter than its diff:
```python
import math

import jax
import jax.numpy as jnp
from jax import lax
from jax.experimental import pallas as pl
from jax.experimental.pallas import tpu as pltpu
from jax.sharding import PartitionSpec as P

H = 32
KV = 4
HD = 128
REQ_REP = 4
PREF_MAX = 512

norm_eps = 1e-05
rope_base = 5000000.0
TQ = 128
KB = 256
NEG_START = -1e30
NEG_MASK = -2e30
CHUNKS = 4


MESH = pl.DeviceIdType.MESH
D = 4096
BLK = 256


def place():
    rep, tp = lax.axis_index("rep"), lax.axis_index("tp")
    return rep, tp, rep // 4, rep % 4, tp // 8, (tp // 2) % 4, tp % 2


def line_order(z):
    power = 1 + 3 * z + 9 * (z * (z - 1) // 2) + 27 * (z * (z - 1) * (z - 2) // 6)
    tables = []
    for picks in ((1, 0, 1, 2), (2, 2, 3, 1), (3, 3, 0, 0)):
        tables.append(sum(pick * 4**i for i, pick in enumerate(picks)))
    return [z] + [(table // power) % 4 for table in tables]


def signal(sem, device):
    pl.semaphore_signal(sem, inc=1, device_id=device, device_id_type=MESH)


class Gather:
    def __init__(self, own, full, recv, send, half):
        self.own, self.full, self.recv, self.send, self.half = own, full, recv, send, half
        self.rep, self.tp, self.x, self.z = place()[:4]
        self.order = line_order(self.z)
        self.right = ((self.x + 1) % 4) * 4
        self.left = ((self.x + 3) % 4) * 4
        self.far = ((self.x + 2) % 4) * 4
        self.pending = []

    def copy(self, src, dst, slot, sem, rep, cond=None):
        made = pltpu.make_async_remote_copy(
            src_ref=src,
            dst_ref=dst,
            send_sem=self.send.at[slot],
            recv_sem=sem,
            device_id=(rep, self.tp),
            device_id_type=MESH,
        )
        if cond is None:
            made.start()
        else:
            pl.when(cond)(made.start)
        self.pending.append((made, cond))

    def arrived(self, index, block):
        ref = self.full.at[block]
        pltpu.make_async_copy(ref, ref, self.recv.at[index, block]).wait()

    def line(self, k):
        zo = self.order[k]
        block = self.x * 4 + zo
        dst, sem = self.full.at[block], self.recv.at[0, block]
        if k == 0:
            src = self.own
            onward, back = self.z < 3, self.z > 0
        else:
            self.arrived(0, block)
            src = dst
            onward, back = (zo < self.z) & (self.z < 3), (zo > self.z) & (self.z > 0)
        self.copy(src, dst, 6 * k, sem, self.x * 4 + lax.min(self.z + 1, 3), onward)
        self.copy(src, dst, 6 * k + 1, sem, self.x * 4 + lax.max(self.z - 1, 0), back)
        self.copy(src, dst, 6 * k + 2, sem, self.right + self.z)
        self.copy(src, dst, 6 * k + 3, sem, self.left + self.z)

    def ring(self, k, side):
        zo = self.order[k]
        block = (self.left if side == 0 else self.right) + zo
        self.arrived(0, block)
        part = pl.ds(0, self.half) if side == 0 else pl.ds(self.half, self.half)
        ref = self.full.at[block, part]
        target = (self.right if side == 0 else self.left) + self.z
        self.copy(ref, ref, 6 * k + 4 + side, self.recv.at[side, block], target)
        return block

    def opposite(self, k):
        block = self.far + self.order[k]
        for side in range(2):
            ref = self.full.at[block, pl.ds(side * self.half, self.half)]
            pltpu.make_async_copy(ref, ref, self.recv.at[side, block]).wait()
        return block

    def drain(self):
        for made, cond in self.pending:
            if cond is None:
                made.wait_send()
            else:
                pl.when(cond)(made.wait_send)


def project_kernel(
    lens_ref, pref_ref, hidden_ref, gain_ref, freq_ref, wq_ref, wkv_ref, wo_ref,
    q_ref, k_ref, v_ref, wo_out,
    hid, x3, full_q, full_s, turned, qacc, kacc, cosine, sine, mine, other,
    hid_sem, recv_q, send_q, recv_s, send_s, kv_send, kv_recv, perm_send, perm_recv, swap_sem, out_sem,
):
    rep, tp, x, z, zh, y, c = place()
    rows = hid.shape[0]
    count = hid_sem.shape[0]
    chunk = rows // count
    loads = []
    for i in range(count):
        at = pl.ds(i * chunk, chunk)
        loads.append(pltpu.make_async_copy(hidden_ref.at[at], hid.at[at], hid_sem.at[i]))
        loads[-1].start()

    zh_t = x // 2
    perm_dst = (y * 4 + zh_t * 2 + c, zh * 8 + ((x % 2) * 2 + z // 2) * 2 + z % 2)
    perm_src = (((z // 2) * 2 + y // 2) * 4 + (y % 2) * 2 + c, zh * 8 + x * 2 + z % 2)
    perm_away = (perm_dst[0] != rep) | (perm_dst[1] != tp)
    barrier = pltpu.get_barrier_semaphore()
    line_right, line_left = x * 4 + lax.min(z + 1, 3), x * 4 + lax.max(z - 1, 0)

    pl.when(z < 3)(lambda: signal(barrier, (line_right, tp)))
    pl.when(z > 0)(lambda: signal(barrier, (line_left, tp)))
    signal(barrier, (((x + 1) % 4) * 4 + z, tp))
    signal(barrier, (((x + 3) % 4) * 4 + z, tp))
    signal(barrier, (rep, tp + 1 - 2 * c))
    pl.when(perm_away)(lambda: signal(barrier, perm_src))
    for j in range(8):
        source = c * 8 + j
        pl.when(source != tp)(lambda source=source: signal(barrier, (rep, source)))
    line_peers = (lax.min(z + 1, 3) - z) + (z - lax.max(z - 1, 0))
    pl.semaphore_wait(barrier, 10 + line_peers + perm_away.astype(jnp.int32) + (c + zh) % 2)

    stream_q = Gather(wq_ref, full_q, recv_q, send_q, BLK // 2)
    stream_s = Gather(full_s.at[rep], full_s, recv_s, send_s, full_s.shape[1] // 2)
    stream_q.line(0)

    wo_dst = full_s.at[perm_dst[0], pl.ds(HD, BLK)]
    permute = pltpu.make_async_remote_copy(
        src_ref=wo_ref, dst_ref=wo_dst, send_sem=perm_send, recv_sem=perm_recv,
        device_id=perm_dst, device_id_type=MESH,
    )
    stay = pltpu.make_async_copy(wo_ref, wo_dst, perm_recv)
    pl.when(perm_away)(permute.start)
    pl.when(jnp.logical_not(perm_away))(stay.start)

    shape = (4 * 16, 4 * 16)
    out_row, in_col = lax.broadcasted_iota(jnp.int32, shape, 0), lax.broadcasted_iota(jnp.int32, shape, 1)
    pick = ((out_row % 16) * KV + out_row // 16 == in_col).astype(jnp.float32).astype(jnp.bfloat16)
    turned[...] = lax.dot_general(
        pick, wkv_ref[...], (((1,), (1,)), ((), ())), preferred_element_type=jnp.float32
    ).astype(jnp.bfloat16)

    starts, first_token = [], 0
    for request in range(REQ_REP):
        starts.append(first_token)
        first_token = first_token + lens_ref[0, request]

    def angles(i, _):
        at = pl.ds(pl.multiple_of(i * 128, 128), 128)
        token = i * 128 + lax.broadcasted_iota(jnp.int32, (128, HD), 0)
        position = jnp.zeros((128, HD), jnp.int32)
        for request in range(REQ_REP):
            shift = pref_ref[request] - starts[request]
            position = jnp.where(token >= starts[request], token + shift, position)
        angle = position.astype(jnp.float32) * freq_ref[...]
        lane = lax.broadcasted_iota(jnp.int32, (128, HD), 1)
        cosine[at, :] = jnp.cos(angle)
        wave = jnp.sin(angle)
        sine[at, :] = jnp.where(lane < HD // 2, -wave, wave)
        return 0

    def norm(i):
        loads[i].wait()

        def some(j, _):
            at = pl.ds(pl.multiple_of(i * chunk + j * 16, 16), 16)
            wide = hid[at, :].astype(jnp.float32)
            meansq = jnp.sum(wide * wide, axis=1, keepdims=True) * (1.0 / D)
            scaled = wide * lax.rsqrt(meansq + norm_eps)
            for b in range(D // BLK):
                cols = slice(b * BLK, (b + 1) * BLK)
                x3[b, at, :] = (scaled[:, cols] * gain_ref[:, cols].astype(jnp.float32)).astype(jnp.bfloat16)
            return 0

        lax.fori_loop(0, chunk // 16, some, 0)

    def piece(head, which):
        target = (head // 2) * 8 + (2 * (head % 2) + which) * 2 + zh
        from_ref = turned.at[pl.ds(head * 16, 16)]
        to_ref = full_s.at[rep, pl.ds(pl.multiple_of((tp % 8) * 16, 16), 16)]
        away = target != tp
        made = pltpu.make_async_remote_copy(
            src_ref=from_ref, dst_ref=to_ref, send_sem=kv_send.at[head * 2 + which], recv_sem=kv_recv.at[tp % 8],
            device_id=(rep, target), device_id_type=MESH,
        )
        here = pltpu.make_async_copy(from_ref, to_ref, kv_recv.at[tp % 8])
        pl.when(away)(made.start)
        pl.when(jnp.logical_not(away))(here.start)
        return made, away

    def use_q(block, own=False):
        for i in range(rows // BLK):
            at = pl.ds(i * BLK, BLK)
            weight = wq_ref[...] if own else full_q[block]
            part = jnp.dot(x3[block, at, :], weight, preferred_element_type=jnp.float32)
            qacc[at, :] = part if own else qacc[at, :] + part

    def use_s(block, own=False):
        for i in range(rows // BLK):
            at = pl.ds(i * BLK, BLK)
            part = lax.dot_general(
                x3[block, at, :], full_s[block, :HD, :], (((1,), (1,)), ((), ())),
                preferred_element_type=jnp.float32,
            )
            kacc[at, :] = part if own else kacc[at, :] + part

    norm(0)
    pieces = [piece(head, which) for head in range(KV) for which in range(2)]
    lax.fori_loop(0, rows // 128, angles, 0)
    norm(1)
    stream_q.line(1)
    norm(2)
    for j in range(8):
        ref = full_s.at[rep, pl.ds(j * 16, 16)]
        pltpu.make_async_copy(ref, ref, kv_recv.at[j]).wait()
    own_wo = full_s.at[rep, pl.ds(HD, BLK)]
    pltpu.make_async_copy(own_wo, own_wo, perm_recv).wait()
    stream_s.line(0)
    norm(3)
    stream_q.line(2)
    norm(4)
    stream_s.line(1)
    norm(5)
    stream_q.line(3)
    norm(6)
    stream_s.line(2)
    norm(7)
    stream_s.line(3)
    use_q(rep, True)
    use_s(rep, True)
    for k in range(4):
        lefts, rights = stream_q.ring(k, 0), stream_q.ring(k, 1)
        lefts_s, rights_s = stream_s.ring(k, 0), stream_s.ring(k, 1)
        if k > 0:
            own_block = x * 4 + stream_q.order[k]
            use_q(own_block)
            use_s(own_block)
        for block in (lefts, rights):
            use_q(block)
        for block in (lefts_s, rights_s):
            use_s(block)
        if k > 0:
            use_q(stream_q.opposite(k - 1))
    use_q(stream_q.opposite(3))
    for k in range(4):
        use_s(stream_s.opposite(k))
    flush = pltpu.make_async_copy(full_s.at[:, pl.ds(HD, BLK)], wo_out, out_sem)
    flush.start()

    fresh = kacc[...].astype(jnp.bfloat16).astype(jnp.float32)
    turned_key = fresh * cosine[...] + pltpu.roll(fresh, HD // 2, 1) * sine[...]
    mine[...] = jnp.where(c == 0, turned_key, fresh).astype(jnp.bfloat16)
    swap = pltpu.make_async_remote_copy(
        src_ref=mine, dst_ref=other, send_sem=swap_sem.at[0], recv_sem=swap_sem.at[1],
        device_id=(rep, tp + 1 - 2 * c), device_id_type=MESH,
    )
    for h in range(q_ref.shape[1] // HD):
        cols = slice(h * HD, (h + 1) * HD)
        u = qacc[:, cols]
        q_ref[:, cols] = (u * cosine[...] + pltpu.roll(u, HD // 2, 1) * sine[...]).astype(jnp.bfloat16)
        if h == 0:
            swap.start()
    for made, away in pieces:
        pl.when(away)(made.wait_send)
    pl.when(perm_away)(permute.wait_send)
    stream_q.drain()
    stream_s.drain()
    swap.wait()

    @pl.when(c == 0)
    def _():
        k_ref[...] = mine[...]
        v_ref[...] = other[...]

    @pl.when(c != 0)
    def _():
        k_ref[...] = other[...]
        v_ref[...] = mine[...]

    flush.wait()


def vmem():
    return pl.BlockSpec(memory_space=pltpu.VMEM)


def smem():
    return pl.BlockSpec(memory_space=pltpu.SMEM)


def anywhere():
    return pl.BlockSpec(memory_space=pl.ANY)


def project(lengths, prefix, hidden, norm_gain, freqs, w_query, w_keyval, w_output):
    rows = hidden.shape[0]
    bf16, f32, dma = jnp.bfloat16, jnp.float32, pltpu.SemaphoreType.DMA
    return pl.pallas_call(
        project_kernel,
        out_shape=(
            jax.ShapeDtypeStruct((rows, BLK), bf16),
            jax.ShapeDtypeStruct((rows, HD), bf16),
            jax.ShapeDtypeStruct((rows, HD), bf16),
            jax.ShapeDtypeStruct((16, BLK, BLK), bf16),
        ),
        in_specs=[smem(), smem(), anywhere(), vmem(), vmem(), vmem(), vmem(), vmem()],
        out_specs=(vmem(), vmem(), vmem(), anywhere()),
        scratch_shapes=[
            pltpu.VMEM((rows, D), bf16),
            pltpu.VMEM((16, rows, BLK), bf16),
            pltpu.VMEM((16, BLK, BLK), bf16),
            pltpu.VMEM((16, HD + BLK, BLK), bf16),
            pltpu.VMEM((64, BLK), bf16),
            pltpu.VMEM((rows, BLK), f32),
            pltpu.VMEM((rows, HD), f32),
            pltpu.VMEM((rows, HD), f32),
            pltpu.VMEM((rows, HD), f32),
            pltpu.VMEM((rows, HD), bf16),
            pltpu.VMEM((rows, HD), bf16),
            dma((8,)),
            dma((2, 16)),
            dma((24,)),
            dma((2, 16)),
            dma((24,)),
            dma((8,)),
            dma((8,)),
            dma,
            dma,
            dma((2,)),
            dma,
        ],
        compiler_params=pltpu.CompilerParams(collective_id=0, has_side_effects=True, vmem_limit_bytes=52 * 2**20),
        cost_estimate=pl.CostEstimate(flops=3 * 10**9, bytes_accessed=12 * 2**20, transcendentals=10**6),
        name="project",
    )(lengths, prefix, hidden, norm_gain, freqs, w_query, w_keyval, w_output)


def attention_kernel(lens_ref, pref_ref, q_ref, k_ref, v_ref, cache_ref, o_ref, stored, m_ref, l_ref, acc_ref, sems):
    kv_head = lax.axis_index("tp") // 4
    column = pl.multiple_of(kv_head * 2 * HD, 2 * HD)
    copies = []
    for request in range(REQ_REP):
        rows = pl.ds(request * PREF_MAX, PREF_MAX)
        copies.append(
            pltpu.make_async_copy(
                cache_ref.at[rows, pl.ds(column, 2 * HD)], stored.at[rows, :], sems.at[request]
            )
        )
        copies[-1].start()
    factor = HD ** (-0.5) * math.log2(math.e)
    heads = q_ref.shape[1] // HD

    def step(q, key, value, mask):
        s = lax.dot_general(q, key, (((1,), (1,)), ((), ())), preferred_element_type=jnp.float32)
        if mask is not None:
            s = jnp.where(mask, s, NEG_MASK)
        old = m_ref[...]
        new = jnp.maximum(old, jnp.max(s, axis=1, keepdims=True))
        shrink = jnp.exp2((old - new) * factor)
        m_ref[...] = new
        p = jnp.exp2((s - new[:, :1]) * factor)
        folded = p[:, :HD]
        for part in range(1, KB // HD):
            folded = folded + p[:, part * HD : (part + 1) * HD]
        l_ref[...] = l_ref[...] * shrink + folded
        acc_ref[...] = acc_ref[...] * shrink + jnp.dot(
            p.astype(jnp.bfloat16), value, preferred_element_type=jnp.float32
        )

    shape = (heads * TQ, KB)
    lane = lax.broadcasted_iota(jnp.int32, shape, 1)
    row = lax.rem(lax.broadcasted_iota(jnp.int32, shape, 0), TQ)
    end = 0
    for request in range(REQ_REP):
        start, prefix = end, pref_ref[request]
        end = start + lens_ref[0, request]
        base = request * PREF_MAX
        copies[request].wait()

        def tile_body(tile, _):
            first = pl.multiple_of(tile * TQ, TQ)
            rows = pl.ds(first, TQ)
            q = jnp.concatenate([q_ref[rows, h * HD : (h + 1) * HD] for h in range(heads)], axis=0)
            m_ref[...] = jnp.full_like(m_ref, NEG_START)
            l_ref[...] = jnp.zeros_like(l_ref)
            acc_ref[...] = jnp.zeros_like(acc_ref)

            def full_block(block, _):
                at = pl.ds(base + pl.multiple_of(block * KB, KB), KB)
                step(q, stored[at, :HD], stored[at, HD:], None)
                return 0

            whole = prefix // KB
            lax.fori_loop(0, whole, full_block, 0)

            @pl.when(whole * KB < prefix)
            def _():
                at = pl.ds(base + pl.multiple_of(whole * KB, KB), KB)
                step(q, stored[at, :HD], stored[at, HD:], lane + whole * KB < prefix)

            def own_block(block, _):
                at = pl.ds(pl.multiple_of(block * KB, KB), KB)
                key_id = lane + block * KB
                step(q, k_ref[at, :], v_ref[at, :], (key_id >= start) & (key_id <= row + first))
                return 0

            def clear_block(block, _):
                at = pl.ds(pl.multiple_of(block * KB, KB), KB)
                step(q, k_ref[at, :], v_ref[at, :], None)
                return 0

            low = start // KB
            high = first // KB
            lax.fori_loop(low, jnp.minimum(low + 1, high), own_block, 0)
            lax.fori_loop(low + 1, high, clear_block, 0)
            own_block(high, 0)
            total = jnp.sum(l_ref[...], axis=1, keepdims=True)
            result = (acc_ref[...] / total).astype(o_ref.dtype)
            tok = first + lax.broadcasted_iota(jnp.int32, (TQ, HD), 0)
            own = (tok >= start) & (tok < end)
            for h in range(heads):
                at = slice(h * HD, (h + 1) * HD)
                o_ref[rows, at] = jnp.where(
                    own, result[h * TQ : (h + 1) * TQ].astype(jnp.float32), o_ref[rows, at].astype(jnp.float32)
                ).astype(o_ref.dtype)
            return 0

        lax.fori_loop(start // TQ, (end - 1) // TQ + 1, tile_body, 0)


def attend(lengths, prefix, q, k, v, cache):
    rows, width = q.shape
    heads = width // HD
    return pl.pallas_call(
        attention_kernel,
        out_shape=jax.ShapeDtypeStruct((rows, width), jnp.bfloat16),
        in_specs=[
            smem(),
            smem(),
            vmem(),
            vmem(),
            vmem(),
            anywhere(),
        ],
        out_specs=vmem(),
        scratch_shapes=[
            pltpu.VMEM((REQ_REP * PREF_MAX, 2 * HD), jnp.bfloat16),
            pltpu.VMEM((heads * TQ, HD), jnp.float32),
            pltpu.VMEM((heads * TQ, HD), jnp.float32),
            pltpu.VMEM((heads * TQ, HD), jnp.float32),
            pltpu.SemaphoreType.DMA((REQ_REP,)),
        ],
        cost_estimate=pl.CostEstimate(flops=2 * 10**9, bytes_accessed=3 * 2**20, transcendentals=2 * 10**6),
        name="attention",
    )(lengths, prefix, q, k, v, cache)


def output_kernel(
    att_ref, hidden_ref, gain_ref, wo_ref,
    resid_ref, normed_ref,
    att, part_send, part_recv, own, hid, sums_mine, sums,
    hid_sem, ring_send, ring_recv, core_send, core_recv, part_sems, sum_send, sum_recv,
):
    rep, tp, x, z, zh, y, c = place()
    rows, width = hid.shape
    load = pltpu.make_async_copy(
        hidden_ref.at[:, pl.ds(pl.multiple_of(tp * width, width), width)], hid, hid_sem
    )
    load.start()
    barrier = pltpu.get_barrier_semaphore()
    for k in range(1, 16):
        signal(barrier, (rep, (tp + k) % 16))
    pl.semaphore_wait(barrier, 15)

    def at_y(to):
        return (rep, zh * 8 + (to % 4) * 2 + c)

    partner = (rep, tp + 1 - 2 * c)
    across = (rep, (tp + 8) % 16)
    size = rows // CHUNKS
    half = size // 2
    pending = []

    def send(src, dst, ssem, rsem, device):
        made = pltpu.make_async_remote_copy(
            src_ref=src, dst_ref=dst, send_sem=ssem, recv_sem=rsem, device_id=device, device_id_type=MESH
        )
        made.start()
        pending.append(made)

    def wait(ref, sem):
        pltpu.make_async_copy(ref, ref, sem).wait()

    def own_send(m):
        at = pl.ds(m * size, size)
        src = att_ref.at[at]
        send(src, att.at[0, 1, at], ring_send.at[0, m], ring_recv.at[0, m], at_y(y + 1))
        send(src, att.at[0, 2, at], ring_send.at[1, m], ring_recv.at[1, m], at_y(y + 3))
        send(src, att.at[1, 0, at], core_send.at[0, m], core_recv.at[0, m], partner)

    def ring_in(m):
        at = pl.ds(m * size, size)
        for side in range(2):
            ref = att.at[0, 1 + side, at]
            wait(ref, ring_recv.at[side, m])
            part = pl.ds(m * size + side * half, half)
            send(
                att.at[0, 1 + side, part], att.at[0, 3, part],
                ring_send.at[2 + side, m], ring_recv.at[2 + side, m], at_y(y + 1 + 2 * side),
            )
            send(ref, att.at[1, 1 + side, at], core_send.at[1 + side, m], core_recv.at[1 + side, m], partner)

    def far_in(m):
        for side in range(2):
            wait(att.at[0, 3, pl.ds(m * size + side * half, half)], ring_recv.at[2 + side, m])
        ref = att.at[0, 3, pl.ds(m * size, size)]
        send(ref, att.at[1, 3, pl.ds(m * size, size)], core_send.at[3, m], core_recv.at[3, m], partner)

    def compute(m):
        at = pl.ds(m * size, size)
        for d in range(4):
            wait(att.at[1, d, at], core_recv.at[d, m])
        for mine in range(2):
            target = zh if mine else 1 - zh
            total = None
            for side in range(2):
                for d, dy in enumerate((0, 3, 1, 2)):
                    core = c if side == 0 else 1 - c
                    block = ((y + dy) % 4) * 4 + target * 2 + core
                    left = att_ref[at, :] if side == 0 and d == 0 else att[side, d, at, :]
                    part = jnp.dot(left, wo_ref[block], preferred_element_type=jnp.float32)
                    total = part if total is None else total + part
            if mine:
                own[at, :] = total
            else:
                part_send[at, :] = total.astype(jnp.bfloat16)
        send(part_send.at[at], part_recv.at[at], part_sems.at[0, m], part_sems.at[1, m], across)

    own_send(0)
    own_send(1)
    for i in range(CHUNKS + 2):
        if i < CHUNKS:
            ring_in(i)
        if i + 2 < CHUNKS:
            own_send(i + 2)
        if 1 <= i <= CHUNKS:
            far_in(i - 1)
        if i >= 2:
            compute(i - 2)
    load.wait()
    for m in range(CHUNKS):
        at = pl.ds(m * size, size)
        wait(part_recv.at[at], part_sems.at[1, m])
        for i in range(size // HD):
            row = m * (size // HD) + i
            here = pl.ds(row * HD, HD)
            resid = (
                hid[here, :].astype(jnp.float32) + (own[here, :] + part_recv[here, :].astype(jnp.float32))
            ).astype(jnp.bfloat16)
            resid_ref[here, :] = resid
            wide = resid.astype(jnp.float32)
            total = jnp.sum(wide * wide, axis=1, keepdims=True)
            sums_mine[pl.ds(row, 1), :] = jnp.transpose(jnp.broadcast_to(total, (HD, HD)))[:1, :]
    for k in range(1, 16):
        send(sums_mine, sums.at[k], sum_send.at[k], sum_recv.at[k], (rep, (tp + k) % 16))
    total = sums_mine[...]
    for k in range(1, 16):
        wait(sums.at[k], sum_recv.at[k])
        total = total + sums[k]
    inverse = lax.rsqrt(total * (1.0 / D) + norm_eps)
    gain = gain_ref[:, pl.ds(pl.multiple_of(tp * width, width), width)].astype(jnp.float32)
    for row in range(rows // HD):
        here = pl.ds(row * HD, HD)
        column = jnp.transpose(jnp.broadcast_to(inverse[row : row + 1, :], (HD, HD)))
        for h in range(width // HD):
            cols = slice(h * HD, (h + 1) * HD)
            normed_ref[here, cols] = (
                resid_ref[here, cols].astype(jnp.float32) * column * gain[:, cols]
            ).astype(jnp.bfloat16)
    for made in pending:
        made.wait_send()


def finish(attended, hidden, out_gain, wo_blocks):
    rows, width = attended.shape
    bf16, f32, dma = jnp.bfloat16, jnp.float32, pltpu.SemaphoreType.DMA
    return pl.pallas_call(
        output_kernel,
        out_shape=(jax.ShapeDtypeStruct((rows, width), bf16), jax.ShapeDtypeStruct((rows, width), bf16)),
        in_specs=[vmem(), anywhere(), vmem(), vmem()],
        out_specs=(vmem(), vmem()),
        scratch_shapes=[
            pltpu.VMEM((2, 4, rows, width), bf16),
            pltpu.VMEM((rows, width), bf16),
            pltpu.VMEM((rows, width), bf16),
            pltpu.VMEM((rows, width), f32),
            pltpu.VMEM((rows, width), bf16),
            pltpu.VMEM((rows // HD, HD), f32),
            pltpu.VMEM((16, rows // HD, HD), f32),
            dma,
            dma((4, CHUNKS)),
            dma((4, CHUNKS)),
            dma((4, CHUNKS)),
            dma((4, CHUNKS)),
            dma((2, CHUNKS)),
            dma((16,)),
            dma((16,)),
        ],
        compiler_params=pltpu.CompilerParams(collective_id=1, has_side_effects=True, vmem_limit_bytes=40 * 2**20),
        cost_estimate=pl.CostEstimate(flops=2 * 10**9, bytes_accessed=6 * 2**20, transcendentals=10**4),
        name="finish",
    )(attended, hidden, out_gain, wo_blocks)


def body(hidden, norm_gain, w_query, w_keyval, w_output, cache, lengths, prefix, out_gain):
    half = HD // 2
    freqs = rope_base ** (-(jnp.arange(half, dtype=jnp.float32) * 2.0 / HD))
    freqs = jnp.concatenate([freqs, freqs]).reshape(1, HD)
    q, k, v, wo_blocks = project(
        lengths, prefix, hidden, norm_gain.reshape(1, -1), freqs, w_query, w_keyval, w_output
    )
    attended = attend(lengths, prefix, q, k, v, cache)
    return finish(attended, hidden, out_gain.reshape(1, -1), wo_blocks)


def solution(mesh):
    placed = (
        P("rep", None),
        P(),
        P("rep", "tp"),
        P("rep", "tp"),
        P("tp", "rep"),
        P("rep", None),
        P("rep", None),
        P("rep"),
        P(),
    )
    return jax.shard_map(
        body,
        mesh=mesh,
        in_specs=placed,
        out_specs=(P("rep", "tp"), P("rep", "tp")),
        check_vma=False,
    )
```

time: 474 us -> 160 us (0.34)
  waiting for transfers between devices: 302 us -> 0 us
  Pallas kernels: 20.4 us -> 143 us
  blocking collectives: 84.4 us -> 0 us
  other arithmetic: 18.6 us -> 0.09 us
  matrix products: 16.1 us -> 0 us
  between operations: 14 us -> 0.71 us
  starting transfers between devices: 6.29 us -> 0 us
    all_gather x4 -> x0, waiting for transfers between devices: 298 us -> none  [the longest x1 125 us: body(): attended_all = lax.all_gather(attended, 'tp', axis=1, tiled=True)]
    pallas_call x0 -> x2, Pallas kernels: none -> 118 us  [the longest x1 69.8 us: project(): pl.pallas_call(project_kernel, out_shape=(jax.ShapeDtypeStruct((rows, BLK...]
    psum x1 -> x0, blocking collectives: 42.4 us -> none  [body(): lax.psum(jnp.sum(wide * wide, axis=-1, keepdims=True), 'tp')]
    all_gather x1 -> x0, blocking collectives: 42 us -> none  [body(): lax.all_gather(w_keyval, 'rep', axis=0, tiled=True)]
    dot_general x3 -> x0, matrix products: 16.1 us -> none  [the longest x1 6.39 us: body(): proj = jnp.dot(attended_all, w_columns, preferred_element_type=jnp.float32)]
    ppermute x1 -> x0, starting transfers between devices: 5.95 us -> none  [body(): lax.ppermute(w_output, ('rep', 'tp'), [(a * tp_count + b, b * tp_count +...]
    reduce_sum x3 -> x0, other arithmetic: 5.38 us -> none  [the longest x1 5.2 us: rms_scale(): meansq = jnp.mean(values * values, axis=-1, keepdims=True)]
    unnamed x21 -> x23, local copies, waits for them, and re-layouts: 6.85 us -> 12.2 us
  transfers between devices with their start and end apart: 5 -> 0, of which waited for: 5 -> 0; matrix products, arithmetic and copies ran while one was open for 6% -> 0% of each run, Pallas kernels for 4% -> 0%
where the time goes in v2:
time: 160 us; the launch traced here: 157 us
  Pallas kernels  143 us (89%)
  local copies, waits for them, and re-layouts  13.6 us (8%)
    pallas_call x1, Pallas kernels, project(): pl.pallas_call(project_kernel, out_shape=(jax.ShapeDtypeStruct((rows, BLK...  69.8 us
    pallas_call x1, Pallas kernels, finish(): pl.pallas_call(output_kernel, out_shape=(jax.ShapeDtypeStruct((rows, widt...  48.7 us
    pallas_call x1, Pallas kernels, attend(): pl.pallas_call(attention_kernel, out_shape=jax.ShapeDtypeStruct((rows, wi...  24.3 us
    unnamed x23, local copies, waits for them, and re-layouts  12.2 us

profile of v2, /device:TPU:1, one launch (start us, length us, event | category | flops | bytes accessed | tf_op | source)
XLA Modules:
  0.0 157.2 jit_solution(2145716213455095846)
XLA Ops:
  0.6 0.1 maximum_bitcast_fusion.freq_ref
  0.7 0.7 reshape.13.gain_ref
  1.4 0.7 reshape.15.gain_ref
  2.1 0.9 copy.11.wkv_ref
  3.0 0.0 copy-start.3
  3.0 0.9 copy-done.3
  3.9 0.0 copy-start.4
  3.9 0.9 copy-done.4
  4.8 0.0 copy-start.5
  4.8 0.7 copy-done.5
  5.5 0.0 copy-start.6
  5.5 0.7 copy-done.6
  6.2 69.8 %project.1 = (bf16[1024,256]{1,0:T(8,128)(2,1)S(1)}, bf16[1024,128]{1,0:T(8,128)(2,1)S(1)}, bf16[1024,128]{1,0:T(8,128)(2,1)S(1)}, bf16[16,256,256]{2,1,0:T(8,128)(2,1)}) custom-call(s32[1,4]{1,0:T(1,128)S(1)} %copy-done.5, s32[4]{0:T(128)S(1)} %copy-done.6, bf16[1024,4096]{1,0:T(8,128)(2,1)} %hidden_ref.3, bf16[1,4096]{1,0:T(2,128)(2,1)S(1)} %reshape.13.gain_ref, ...), custom_call_target="tpu_custom_call" | custom-call | flops 3000000000 | bytes 12582912 | tf_op jit(solution)/shard_map/project/pallas_call | solution.py:327
  76.0 0.0 copy-start.7
  76.0 0.8 copy-done.7
  76.8 0.0 copy-start.8
  76.8 0.7 copy-done.8
  77.5 0.0 copy-start.9
  77.5 0.7 copy-done.9
  78.2 0.0 copy-start.1
  78.2 24.3 %attention.1.att_ref = bf16[1024,256]{1,0:T(8,128)(2,1)} custom-call(s32[1,4]{1,0:T(1,128)} %lens_ref.3, s32[4]{0:T(128)} %pref_ref.3, bf16[1024,256]{1,0:T(8,128)(2,1)} %copy-done.7, bf16[1024,128]{1,0:T(8,128)(2,1)} %copy-done.8, bf16[1024,128]{1,0:T(8,128)(2,1)} %copy-done.9, bf16[2048,1024]{1,0:T(8,128)(2,1)} %cache_ref.1), custom_call_target="tpu_custom_call" | custom-call | flops 2000000000 | bytes 3145728 | tf_op jit(solution)/shard_map/attention/pallas_call | solution.py:463
  102.5 0.0 copy-done.1
  102.5 0.0 copy-start
  102.6 3.4 %copy-done = bf16[1024,4096]{1,0:T(8,128)(2,1)S(1)} copy-done((bf16[1024,4096]{1,0:T(8,128)(2,1)S(1)}, bf16[1024,4096]{1,0:T(8,128)(2,1)}, u32[]{:S(2)}) %copy-start) | copy-done | bytes 8388632
  105.9 0.0 copy-start.2
  105.9 1.0 copy-done.2
  107.0 48.7 %finish.1 = (bf16[1024,256]{1,0:T(8,128)(2,1)S(1)}, bf16[1024,256]{1,0:T(8,128)(2,1)S(1)}) custom-call(bf16[1024,256]{1,0:T(8,128)(2,1)S(1)} %copy-done.2, bf16[1024,4096]{1,0:T(8,128)(2,1)S(1)} %copy-done, bf16[1,4096]{1,0:T(2,128)(2,1)S(1)} %reshape.15.gain_ref, bf16[16,256,256]{2,1,0:T(8,128)(2,1)S(1)} %copy-done.1), custom_call_target="tpu_custom_call" | custom-call | flops 2000000000 | bytes 6291456 | tf_op jit(solution)/shard_map/finish/pallas_call | solution.py:616
  155.6 0.8 copy.14
  156.4 0.8 copy.15
  (1 shorter events, 0.0 us)
Async XLA Ops:
  3.0 0.9 copy-start.3
  3.9 0.9 copy-start.4
  4.8 0.7 copy-start.5
  5.5 0.7 copy-start.6
  76.0 0.8 copy-start.7
  76.8 0.7 copy-start.8
  77.5 0.7 copy-start.9
  78.2 24.4 %copy-start.1 = (bf16[16,256,256]{2,1,0:T(8,128)(2,1)S(1)}, bf16[16,256,256]{2,1,0:T(8,128)(2,1)}, u32[]{:S(2)}) copy-start(bf16[16,256,256]{2,1,0:T(8,128)(2,1)} %get-tuple-element.9.wo_ref) | copy-start | bytes 6291460
  102.5 3.4 %copy-start = (bf16[1024,4096]{1,0:T(8,128)(2,1)S(1)}, bf16[1024,4096]{1,0:T(8,128)(2,1)}, u32[]{:S(2)}) copy-start(bf16[1024,4096]{1,0:T(8,128)(2,1)} %hidden_ref.3) | copy-start | bytes 25165828
  105.9 1.0 copy-start.2

commit v3 on v2

--- a/solution.py
+++ b/solution.py
@@ -1,7 +1,9 @@
+import functools
 import math
 
 import jax
 import jax.numpy as jnp
+import numpy as np
 from jax import lax
 from jax.experimental import pallas as pl
 from jax.experimental.pallas import tpu as pltpu
@@ -15,10 +17,9 @@
 
 norm_eps = 1e-05
 rope_base = 5000000.0
-TQ = 128
-KB = 256
-NEG_START = -1e30
-NEG_MASK = -2e30
+TQ = 256
+NEG_MASK = -1e30
+VMEM_ALL = 67043328
 CHUNKS = 4
 
 
@@ -116,9 +117,9 @@
 
 def project_kernel(
     lens_ref, pref_ref, hidden_ref, gain_ref, freq_ref, wq_ref, wkv_ref, wo_ref,
-    q_ref, k_ref, v_ref, wo_out,
-    hid, x3, full_q, full_s, turned, qacc, kacc, cosine, sine, mine, other,
-    hid_sem, recv_q, send_q, recv_s, send_s, kv_send, kv_recv, perm_send, perm_recv, swap_sem, out_sem,
+    q_out, k_out, v_out, wo_out,
+    gain, q_ref, k_ref, v_ref, hid, x3, full_q, full_s, turned, qacc, kacc, cosine, sine, mine, other,
+    hid_sem, recv_q, send_q, recv_s, send_s, kv_send, kv_recv, perm_send, perm_recv, swap_sem, out_sem, own_sem, store_sem,
 ):
     rep, tp, x, z, zh, y, c = place()
     rows = hid.shape[0]
@@ -129,6 +130,8 @@
         at = pl.ds(i * chunk, chunk)
         loads.append(pltpu.make_async_copy(hidden_ref.at[at], hid.at[at], hid_sem.at[i]))
         loads[-1].start()
+    own_load = pltpu.make_async_copy(wq_ref, full_q.at[rep], own_sem)
+    own_load.start()
 
     zh_t = x // 2
     perm_dst = (y * 4 + zh_t * 2 + c, zh * 8 + ((x % 2) * 2 + z // 2) * 2 + z % 2)
@@ -166,7 +169,7 @@
     out_row, in_col = lax.broadcasted_iota(jnp.int32, shape, 0), lax.broadcasted_iota(jnp.int32, shape, 1)
     pick = ((out_row % 16) * KV + out_row // 16 == in_col).astype(jnp.float32).astype(jnp.bfloat16)
     turned[...] = lax.dot_general(
-        pick, wkv_ref[...], (((1,), (1,)), ((), ())), preferred_element_type=jnp.float32
+        pick, wkv_ref[...], (((1,), (0,)), ((), ())), preferred_element_type=jnp.float32
     ).astype(jnp.bfloat16)
 
     starts, first_token = [], 0
@@ -188,6 +191,8 @@
         sine[at, :] = jnp.where(lane < HD // 2, -wave, wave)
         return 0
 
+    gain[...] = gain_ref[...].astype(jnp.float32).reshape(1, D)
+
     def norm(i):
         loads[i].wait()
 
@@ -198,7 +203,7 @@
             scaled = wide * lax.rsqrt(meansq + norm_eps)
             for b in range(D // BLK):
                 cols = slice(b * BLK, (b + 1) * BLK)
-                x3[b, at, :] = (scaled[:, cols] * gain_ref[:, cols].astype(jnp.float32)).astype(jnp.bfloat16)
+                x3[b, at, :] = (scaled[:, cols] * gain[:, cols]).astype(jnp.bfloat16)
             return 0
 
         lax.fori_loop(0, chunk // 16, some, 0)
@@ -220,8 +225,7 @@
     def use_q(block, own=False):
         for i in range(rows // BLK):
             at = pl.ds(i * BLK, BLK)
-            weight = wq_ref[...] if own else full_q[block]
-            part = jnp.dot(x3[block, at, :], weight, preferred_element_type=jnp.float32)
+            part = jnp.dot(x3[block, at, :], full_q[block], preferred_element_type=jnp.float32)
             qacc[at, :] = part if own else qacc[at, :] + part
 
     def use_s(block, own=False):
@@ -255,6 +259,7 @@
     stream_s.line(2)
     norm(7)
     stream_s.line(3)
+    own_load.wait()
     use_q(rep, True)
     use_s(rep, True)
     for k in range(4):
@@ -289,6 +294,8 @@
         q_ref[:, cols] = (u * cosine[...] + pltpu.roll(u, HD // 2, 1) * sine[...]).astype(jnp.bfloat16)
         if h == 0:
             swap.start()
+    store_q = pltpu.make_async_copy(q_ref, q_out, store_sem.at[0])
+    store_q.start()
     for made, away in pieces:
         pl.when(away)(made.wait_send)
     pl.when(perm_away)(permute.wait_send)
@@ -306,6 +313,13 @@
         k_ref[...] = other[...]
         v_ref[...] = mine[...]
 
+    store_k = pltpu.make_async_copy(k_ref, k_out, store_sem.at[1])
+    store_v = pltpu.make_async_copy(v_ref, v_out, store_sem.at[2])
+    store_k.start()
+    store_v.start()
+    store_q.wait()
+    store_k.wait()
+    store_v.wait()
     flush.wait()
 
 
@@ -332,9 +346,13 @@
             jax.ShapeDtypeStruct((rows, HD), bf16),
             jax.ShapeDtypeStruct((16, BLK, BLK), bf16),
         ),
-        in_specs=[smem(), smem(), anywhere(), vmem(), vmem(), vmem(), vmem(), vmem()],
-        out_specs=(vmem(), vmem(), vmem(), anywhere()),
+        in_specs=[smem(), smem(), anywhere(), vmem(), vmem(), anywhere(), vmem(), anywhere()],
+        out_specs=(anywhere(), anywhere(), anywhere(), anywhere()),
         scratch_shapes=[
+            pltpu.VMEM((1, D), f32),
+            pltpu.VMEM((rows, BLK), bf16),
+            pltpu.VMEM((rows, HD), bf16),
+            pltpu.VMEM((rows, HD), bf16),
             pltpu.VMEM((rows, D), bf16),
             pltpu.VMEM((16, rows, BLK), bf16),
             pltpu.VMEM((16, BLK, BLK), bf16),
@@ -357,138 +375,131 @@
             dma,
             dma((2,)),
             dma,
+            dma,
+            dma((3,)),
         ],
-        compiler_params=pltpu.CompilerParams(collective_id=0, has_side_effects=True, vmem_limit_bytes=52 * 2**20),
+        compiler_params=pltpu.CompilerParams(collective_id=0, has_side_effects=True, vmem_limit_bytes=VMEM_ALL),
         cost_estimate=pl.CostEstimate(flops=3 * 10**9, bytes_accessed=12 * 2**20, transcendentals=10**6),
         name="project",
     )(lengths, prefix, hidden, norm_gain, freqs, w_query, w_keyval, w_output)
 
 
-def attention_kernel(lens_ref, pref_ref, q_ref, k_ref, v_ref, cache_ref, o_ref, stored, m_ref, l_ref, acc_ref, sems):
-    kv_head = lax.axis_index("tp") // 4
-    column = pl.multiple_of(kv_head * 2 * HD, 2 * HD)
-    copies = []
-    for request in range(REQ_REP):
-        rows = pl.ds(request * PREF_MAX, PREF_MAX)
-        copies.append(
-            pltpu.make_async_copy(
-                cache_ref.at[rows, pl.ds(column, 2 * HD)], stored.at[rows, :], sems.at[request]
-            )
-        )
-        copies[-1].start()
+def attention_kernel(
+    lens_ref, pref_ref, q_ref, k_ref, v_ref, cache_ref, o_ref, qs, ks, vs, stored, outs, sems, out_sem
+):
+    rows, width = q_ref.shape
+    column = pl.multiple_of(lax.axis_index("tp") // 4 * 2 * HD, 2 * HD)
+    inside = pl.ds(0, rows)
+    loads = [
+        pltpu.make_async_copy(q_ref, qs.at[inside], sems.at[REQ_REP]),
+        pltpu.make_async_copy(k_ref, ks.at[inside], sems.at[REQ_REP + 1]),
+        pltpu.make_async_copy(v_ref, vs.at[inside], sems.at[REQ_REP + 2]),
+    ]
+
+    def fetch(request):
+        at = pl.ds(pl.multiple_of(request * PREF_MAX, PREF_MAX), PREF_MAX)
+        return pltpu.make_async_copy(cache_ref.at[at, pl.ds(column, 2 * HD)], stored.at[at, :], sems.at[request])
+
+    fetch(0).start()
+    for load in loads:
+        load.start()
+    for request in range(1, REQ_REP):
+        fetch(request).start()
+    spare = pl.ds(rows, qs.shape[0] - rows)
+    ks[spare, :] = jnp.zeros((TQ, HD), jnp.bfloat16)
+    vs[spare, :] = jnp.zeros((TQ, HD), jnp.bfloat16)
+    for load in loads:
+        load.wait()
     factor = HD ** (-0.5) * math.log2(math.e)
-    heads = q_ref.shape[1] // HD
-
-    def step(q, key, value, mask):
-        s = lax.dot_general(q, key, (((1,), (1,)), ((), ())), preferred_element_type=jnp.float32)
-        if mask is not None:
-            s = jnp.where(mask, s, NEG_MASK)
-        old = m_ref[...]
-        new = jnp.maximum(old, jnp.max(s, axis=1, keepdims=True))
-        shrink = jnp.exp2((old - new) * factor)
-        m_ref[...] = new
-        p = jnp.exp2((s - new[:, :1]) * factor)
-        folded = p[:, :HD]
-        for part in range(1, KB // HD):
-            folded = folded + p[:, part * HD : (part + 1) * HD]
-        l_ref[...] = l_ref[...] * shrink + folded
-        acc_ref[...] = acc_ref[...] * shrink + jnp.dot(
-            p.astype(jnp.bfloat16), value, preferred_element_type=jnp.float32
-        )
-
-    shape = (heads * TQ, KB)
-    lane = lax.broadcasted_iota(jnp.int32, shape, 1)
-    row = lax.rem(lax.broadcasted_iota(jnp.int32, shape, 0), TQ)
-    end = 0
-    for request in range(REQ_REP):
-        start, prefix = end, pref_ref[request]
-        end = start + lens_ref[0, request]
+    nt = (((1,), (1,)), ((), ()))
+    lane = lax.broadcasted_iota(jnp.int32, (TQ, TQ), 1)
+    row = lax.broadcasted_iota(jnp.int32, (TQ, TQ), 0)
+
+    def tile(start, aligned, base, prefix, index, parts):
+        rows_at = pl.ds(pl.multiple_of(aligned + index * TQ, 16), TQ)
+        for h in range(width // HD):
+            cols = slice(h * HD, (h + 1) * HD)
+            q = qs[rows_at, cols]
+            scores, values = [], []
+            for part in range(parts):
+                at = pl.ds(pl.multiple_of(base + part * TQ, TQ), TQ)
+                score = lax.dot_general(q, stored[at, :HD], nt, preferred_element_type=jnp.float32)
+                if part == parts - 1:
+                    score = jnp.where(lane < prefix - part * TQ, score, NEG_MASK)
+                scores.append(score)
+                values.append((stored, at, slice(HD, 2 * HD)))
+            for part in range(index + 1):
+                at = pl.ds(pl.multiple_of(aligned + part * TQ, 16), TQ)
+                score = lax.dot_general(q, ks[at, :], nt, preferred_element_type=jnp.float32)
+                if part == index:
+                    score = jnp.where(lane <= row, score, NEG_MASK)
+                if part == 0:
+                    score = jnp.where(lane >= start - aligned, score, NEG_MASK)
+                scores.append(score)
+                values.append((vs, at, slice(0, HD)))
+            peak = scores[0]
+            for score in scores[1:]:
+                peak = jnp.maximum(peak, score)
+            peak = jnp.max(peak, axis=1, keepdims=True)
+            total, gathered = None, None
+            for score, (ref, at, which) in zip(scores, values):
+                e = jnp.exp2((score - peak) * factor)
+                total = e if total is None else total + e
+                part = jnp.dot(e.astype(jnp.bfloat16), ref[at, which], preferred_element_type=jnp.float32)
+                gathered = part if gathered is None else gathered + part
+            result = gathered / jnp.sum(total, axis=1, keepdims=True)
+            if index == 0:
+                keep = row[:, :HD] + aligned < start
+                result = jnp.where(keep, outs[rows_at, cols].astype(jnp.float32), result)
+            outs[rows_at, cols] = result.astype(jnp.bfloat16)
+
+    def one(request, start):
+        end, prefix = start + lens_ref[0, request], pref_ref[request]
+        aligned = start // 16 * 16
         base = request * PREF_MAX
-        copies[request].wait()
-
-        def tile_body(tile, _):
-            first = pl.multiple_of(tile * TQ, TQ)
-            rows = pl.ds(first, TQ)
-            q = jnp.concatenate([q_ref[rows, h * HD : (h + 1) * HD] for h in range(heads)], axis=0)
-            m_ref[...] = jnp.full_like(m_ref, NEG_START)
-            l_ref[...] = jnp.zeros_like(l_ref)
-            acc_ref[...] = jnp.zeros_like(acc_ref)
-
-            def full_block(block, _):
-                at = pl.ds(base + pl.multiple_of(block * KB, KB), KB)
-                step(q, stored[at, :HD], stored[at, HD:], None)
-                return 0
-
-            whole = prefix // KB
-            lax.fori_loop(0, whole, full_block, 0)
-
-            @pl.when(whole * KB < prefix)
-            def _():
-                at = pl.ds(base + pl.multiple_of(whole * KB, KB), KB)
-                step(q, stored[at, :HD], stored[at, HD:], lane + whole * KB < prefix)
-
-            def own_block(block, _):
-                at = pl.ds(pl.multiple_of(block * KB, KB), KB)
-                key_id = lane + block * KB
-                step(q, k_ref[at, :], v_ref[at, :], (key_id >= start) & (key_id <= row + first))
-                return 0
-
-            def clear_block(block, _):
-                at = pl.ds(pl.multiple_of(block * KB, KB), KB)
-                step(q, k_ref[at, :], v_ref[at, :], None)
-                return 0
-
-            low = start // KB
-            high = first // KB
-            lax.fori_loop(low, jnp.minimum(low + 1, high), own_block, 0)
-            lax.fori_loop(low + 1, high, clear_block, 0)
-            own_block(high, 0)
-            total = jnp.sum(l_ref[...], axis=1, keepdims=True)
-            result = (acc_ref[...] / total).astype(o_ref.dtype)
-            tok = first + lax.broadcasted_iota(jnp.int32, (TQ, HD), 0)
-            own = (tok >= start) & (tok < end)
-            for h in range(heads):
-                at = slice(h * HD, (h + 1) * HD)
-                o_ref[rows, at] = jnp.where(
-                    own, result[h * TQ : (h + 1) * TQ].astype(jnp.float32), o_ref[rows, at].astype(jnp.float32)
-                ).astype(o_ref.dtype)
-            return 0
-
-        lax.fori_loop(start // TQ, (end - 1) // TQ + 1, tile_body, 0)
+        fetch(request).wait()
+        for index in range(3):
+            for parts in (1, 2):
+                fits = (prefix <= TQ) if parts == 1 else (prefix > TQ)
+                pl.when((aligned + index * TQ < end) & fits)(
+                    functools.partial(tile, start, aligned, base, prefix, index, parts)
+                )
+        return end
+
+    lax.fori_loop(0, REQ_REP, one, 0)
+    store = pltpu.make_async_copy(outs.at[inside], o_ref, out_sem)
+    store.start()
+    store.wait()
 
 
 def attend(lengths, prefix, q, k, v, cache):
     rows, width = q.shape
-    heads = width // HD
+    bf16, dma = jnp.bfloat16, pltpu.SemaphoreType.DMA
     return pl.pallas_call(
         attention_kernel,
-        out_shape=jax.ShapeDtypeStruct((rows, width), jnp.bfloat16),
-        in_specs=[
-            smem(),
-            smem(),
-            vmem(),
-            vmem(),
-            vmem(),
-            anywhere(),
+        out_shape=jax.ShapeDtypeStruct((rows, width), bf16),
+        in_specs=[smem(), smem(), anywhere(), anywhere(), anywhere(), anywhere()],
+        out_specs=anywhere(),
+        scratch_shapes=[
+            pltpu.VMEM((rows + TQ, width), bf16),
+            pltpu.VMEM((rows + TQ, HD), bf16),
+            pltpu.VMEM((rows + TQ, HD), bf16),
+            pltpu.VMEM((REQ_REP * PREF_MAX, 2 * HD), bf16),
+            pltpu.VMEM((rows + TQ, width), bf16),
+            dma((REQ_REP + 3,)),
+            dma,
         ],
-        out_specs=vmem(),
-        scratch_shapes=[
-            pltpu.VMEM((REQ_REP * PREF_MAX, 2 * HD), jnp.bfloat16),
-            pltpu.VMEM((heads * TQ, HD), jnp.float32),
-            pltpu.VMEM((heads * TQ, HD), jnp.float32),
-            pltpu.VMEM((heads * TQ, HD), jnp.float32),
-            pltpu.SemaphoreType.DMA((REQ_REP,)),
-        ],
+        compiler_params=pltpu.CompilerParams(vmem_limit_bytes=VMEM_ALL),
         cost_estimate=pl.CostEstimate(flops=2 * 10**9, bytes_accessed=3 * 2**20, transcendentals=2 * 10**6),
         name="attention",
     )(lengths, prefix, q, k, v, cache)
 
 
 def output_kernel(
-    att_ref, hidden_ref, gain_ref, wo_ref,
+    att_ref, hidden_ref, gain_ref, wo_in,
     resid_ref, normed_ref,
-    att, part_send, part_recv, own, hid, sums_mine, sums,
-    hid_sem, ring_send, ring_recv, core_send, core_recv, part_sems, sum_send, sum_recv,
+    gain_row, wo_ref, att, part_send, part_recv, own, hid, sums_mine, sums,
+    hid_sem, ring_send, ring_recv, core_send, core_recv, part_sems, sum_send, sum_recv, wo_sem, own_sem,
 ):
     rep, tp, x, z, zh, y, c = place()
     rows, width = hid.shape
@@ -496,6 +507,11 @@
         hidden_ref.at[:, pl.ds(pl.multiple_of(tp * width, width), width)], hid, hid_sem
     )
     load.start()
+    load_wo = pltpu.make_async_copy(wo_in, wo_ref, wo_sem)
+    load_wo.start()
+    load_own = pltpu.make_async_copy(att_ref, att.at[0, 0], own_sem)
+    load_own.start()
+    gain_row[...] = gain_ref[...].astype(jnp.float32).reshape(1, D)
     barrier = pltpu.get_barrier_semaphore()
     for k in range(1, 16):
         signal(barrier, (rep, (tp + k) % 16))
@@ -556,7 +572,7 @@
                 for d, dy in enumerate((0, 3, 1, 2)):
                     core = c if side == 0 else 1 - c
                     block = ((y + dy) % 4) * 4 + target * 2 + core
-                    left = att_ref[at, :] if side == 0 and d == 0 else att[side, d, at, :]
+                    left = att[side, d, at, :]
                     part = jnp.dot(left, wo_ref[block], preferred_element_type=jnp.float32)
                     total = part if total is None else total + part
             if mine:
@@ -567,6 +583,8 @@
 
     own_send(0)
     own_send(1)
+    load_wo.wait()
+    load_own.wait()
     for i in range(CHUNKS + 2):
         if i < CHUNKS:
             ring_in(i)
@@ -597,7 +615,7 @@
         wait(sums.at[k], sum_recv.at[k])
         total = total + sums[k]
     inverse = lax.rsqrt(total * (1.0 / D) + norm_eps)
-    gain = gain_ref[:, pl.ds(pl.multiple_of(tp * width, width), width)].astype(jnp.float32)
+    gain = gain_row[:, pl.ds(pl.multiple_of(tp * width, width), width)]
     for row in range(rows // HD):
         here = pl.ds(row * HD, HD)
         column = jnp.transpose(jnp.broadcast_to(inverse[row : row + 1, :], (HD, HD)))
@@ -616,9 +634,11 @@
     return pl.pallas_call(
         output_kernel,
         out_shape=(jax.ShapeDtypeStruct((rows, width), bf16), jax.ShapeDtypeStruct((rows, width), bf16)),
-        in_specs=[vmem(), anywhere(), vmem(), vmem()],
+        in_specs=[anywhere(), anywhere(), vmem(), anywhere()],
         out_specs=(vmem(), vmem()),
         scratch_shapes=[
+            pltpu.VMEM((1, D), f32),
+            pltpu.VMEM((16, BLK, BLK), bf16),
             pltpu.VMEM((2, 4, rows, width), bf16),
             pltpu.VMEM((rows, width), bf16),
             pltpu.VMEM((rows, width), bf16),
@@ -634,22 +654,21 @@
             dma((2, CHUNKS)),
             dma((16,)),
             dma((16,)),
+            dma,
+            dma,
         ],
-        compiler_params=pltpu.CompilerParams(collective_id=1, has_side_effects=True, vmem_limit_bytes=40 * 2**20),
+        compiler_params=pltpu.CompilerParams(collective_id=1, has_side_effects=True, vmem_limit_bytes=VMEM_ALL),
         cost_estimate=pl.CostEstimate(flops=2 * 10**9, bytes_accessed=6 * 2**20, transcendentals=10**4),
         name="finish",
     )(attended, hidden, out_gain, wo_blocks)
 
 
 def body(hidden, norm_gain, w_query, w_keyval, w_output, cache, lengths, prefix, out_gain):
-    half = HD // 2
-    freqs = rope_base ** (-(jnp.arange(half, dtype=jnp.float32) * 2.0 / HD))
-    freqs = jnp.concatenate([freqs, freqs]).reshape(1, HD)
-    q, k, v, wo_blocks = project(
-        lengths, prefix, hidden, norm_gain.reshape(1, -1), freqs, w_query, w_keyval, w_output
-    )
+    powers = np.arange(HD) % (HD // 2) * 2.0 / HD
+    freqs = jnp.asarray((rope_base**-powers).astype(np.float32).reshape(1, HD))
+    q, k, v, wo_blocks = project(lengths, prefix, hidden, norm_gain, freqs, w_query, w_keyval.T, w_output)
     attended = attend(lengths, prefix, q, k, v, cache)
-    return finish(attended, hidden, out_gain.reshape(1, -1), wo_blocks)
+    return finish(attended, hidden, out_gain, wo_blocks)
 
 
 def solution(mesh):

time: 160 us -> 140 us (0.88); the launches traced: 157 us -> 140 us
  local copies, waits for them, and re-layouts: 13.6 us -> 3.74 us
  Pallas kernels: 143 us -> 136 us
    pallas_call x1, Pallas kernels: 24.3 us -> 9.44 us  [attend(): pl.pallas_call(attention_kernel, out_shape=jax.ShapeDtypeStruct((rows, wi...]
    unnamed x23 -> x2, local copies, waits for them, and re-layouts: 12.2 us -> 3.74 us
    pallas_call x1, Pallas kernels: 48.7 us -> 54.8 us  [finish(): pl.pallas_call(output_kernel, out_shape=(jax.ShapeDtypeStruct((rows, widt...]
where the time goes in v3:
time: 140 us
  Pallas kernels  136 us (97%)
  local copies, waits for them, and re-layouts  3.74 us (3%)
    pallas_call x1, Pallas kernels, project(): pl.pallas_call(project_kernel, out_shape=(jax.ShapeDtypeStruct((rows, BLK...  71.4 us
    pallas_call x1, Pallas kernels, finish(): pl.pallas_call(output_kernel, out_shape=(jax.ShapeDtypeStruct((rows, widt...  54.8 us
    pallas_call x1, Pallas kernels, attend(): pl.pallas_call(attention_kernel, out_shape=jax.ShapeDtypeStruct((rows, wi...  9.44 us
    unnamed x2, local copies, waits for them, and re-layouts  3.74 us

profile of v3, /device:TPU:1, one launch (start us, length us, event | category | flops | bytes accessed | tf_op | source)
XLA Modules:
  0.0 140.0 jit_solution(11528679741822232170)
XLA Ops:
  0.6 71.4 %project.1 = (bf16[1024,256]{1,0:T(8,128)(2,1)}, bf16[1024,128]{1,0:T(8,128)(2,1)}, bf16[1024,128]{1,0:T(8,128)(2,1)}, bf16[16,256,256]{2,1,0:T(8,128)(2,1)}) custom-call(s32[1,4]{1,0:T(1,128)} %lens_ref.3, s32[4]{0:T(128)} %pref_ref.3, bf16[1024,4096]{1,0:T(8,128)(2,1)} %hidden_ref.3, bf16[4096]{0:T(1024)(128)(2,1)} %gain_ref.2, ...), custom_call_target="tpu_custom_call" | custom-call | flops 3000000000 | bytes 12582912 | tf_op jit(solution)/shard_map/project/pallas_call | solution.py:341
  72.0 9.4 %attention.1.att_ref = bf16[1024,256]{1,0:T(8,128)(2,1)} custom-call(s32[1,4]{1,0:T(1,128)} %lens_ref.3, s32[4]{0:T(128)} %pref_ref.3, bf16[1024,256]{1,0:T(8,128)(2,1)} %get-tuple-element.6.q_ref, bf16[1024,128]{1,0:T(8,128)(2,1)} %get-tuple-element.7.k_ref, bf16[1024,128]{1,0:T(8,128)(2,1)} %get-tuple-element.8.v_ref, bf16[2048,1024]{1,0:T(8,128)(2,1)} %cache_ref.1), custom_call_target="tpu_custom_call" | custom-call | flops 2000000000 | bytes 3145728 | tf_op jit(solution)/shard_map/attention/pallas_call | solution.py:478
  81.5 54.8 %finish.1 = (bf16[1024,256]{1,0:T(8,128)(2,1)}, bf16[1024,256]{1,0:T(8,128)(2,1)}) custom-call(bf16[1024,256]{1,0:T(8,128)(2,1)} %attention.1.att_ref, bf16[1024,4096]{1,0:T(8,128)(2,1)} %hidden_ref.3, bf16[4096]{0:T(1024)(128)(2,1)} %gain_ref.3, bf16[16,256,256]{2,1,0:T(8,128)(2,1)} %get-tuple-element.9.wo_in), custom_call_target="tpu_custom_call" | custom-call | flops 2000000000 | bytes 6291456 | tf_op jit(solution)/shard_map/finish/pallas_call | solution.py:634
  136.2 1.9 %copy.14 = bf16[1024,256]{1,0:T(8,128)(2,1)} copy(bf16[1024,256]{1,0:T(8,128)(2,1)} %get-tuple-element.12) | data formatting | bytes 1048576
  138.1 1.9 %copy.15 = bf16[1024,256]{1,0:T(8,128)(2,1)} copy(bf16[1024,256]{1,0:T(8,128)(2,1)} %get-tuple-element.13) | data formatting | bytes 1048576

commit v4 on v3

--- a/solution.py
+++ b/solution.py
@@ -20,7 +20,9 @@
 TQ = 256
 NEG_MASK = -1e30
 VMEM_ALL = 67043328
-CHUNKS = 4
+CHUNKS = 8
+WEIGHT_AT = 3
+OWN_EARLY = 3
 
 
 MESH = pl.DeviceIdType.MESH
@@ -46,8 +48,9 @@
 
 
 class Gather:
-    def __init__(self, own, full, recv, send, half):
+    def __init__(self, own, full, recv, send, half, ring=True):
         self.own, self.full, self.recv, self.send, self.half = own, full, recv, send, half
+        self.in_ring = ring
         self.rep, self.tp, self.x, self.z = place()[:4]
         self.order = line_order(self.z)
         self.right = ((self.x + 1) % 4) * 4
@@ -76,7 +79,7 @@
 
     def line(self, k):
         zo = self.order[k]
-        block = self.x * 4 + zo
+        block = self.x * 4 + zo if self.in_ring else zo
         dst, sem = self.full.at[block], self.recv.at[0, block]
         if k == 0:
             src = self.own
@@ -87,6 +90,8 @@
             onward, back = (zo < self.z) & (self.z < 3), (zo > self.z) & (self.z > 0)
         self.copy(src, dst, 6 * k, sem, self.x * 4 + lax.min(self.z + 1, 3), onward)
         self.copy(src, dst, 6 * k + 1, sem, self.x * 4 + lax.max(self.z - 1, 0), back)
+        if not self.in_ring:
+            return
         self.copy(src, dst, 6 * k + 2, sem, self.right + self.z)
         self.copy(src, dst, 6 * k + 3, sem, self.left + self.z)
 
@@ -118,8 +123,8 @@
 def project_kernel(
     lens_ref, pref_ref, hidden_ref, gain_ref, freq_ref, wq_ref, wkv_ref, wo_ref,
     q_out, k_out, v_out, wo_out,
-    gain, q_ref, k_ref, v_ref, hid, x3, full_q, full_s, turned, qacc, kacc, cosine, sine, mine, other,
-    hid_sem, recv_q, send_q, recv_s, send_s, kv_send, kv_recv, perm_send, perm_recv, swap_sem, out_sem, own_sem, store_sem,
+    gain, q_ref, k_ref, v_ref, hid, x3, full_q, full_s, full_w, turned, qacc, kacc, cosine, sine, mine, other,
+    hid_sem, recv_q, send_q, recv_s, send_s, recv_w, send_w, kv_send, kv_recv, perm_send, perm_recv, swap_sem, out_sem, own_sem, store_sem,
 ):
     rep, tp, x, z, zh, y, c = place()
     rows = hid.shape[0]
@@ -149,22 +154,6 @@
     for j in range(8):
         source = c * 8 + j
         pl.when(source != tp)(lambda source=source: signal(barrier, (rep, source)))
-    line_peers = (lax.min(z + 1, 3) - z) + (z - lax.max(z - 1, 0))
-    pl.semaphore_wait(barrier, 10 + line_peers + perm_away.astype(jnp.int32) + (c + zh) % 2)
-
-    stream_q = Gather(wq_ref, full_q, recv_q, send_q, BLK // 2)
-    stream_s = Gather(full_s.at[rep], full_s, recv_s, send_s, full_s.shape[1] // 2)
-    stream_q.line(0)
-
-    wo_dst = full_s.at[perm_dst[0], pl.ds(HD, BLK)]
-    permute = pltpu.make_async_remote_copy(
-        src_ref=wo_ref, dst_ref=wo_dst, send_sem=perm_send, recv_sem=perm_recv,
-        device_id=perm_dst, device_id_type=MESH,
-    )
-    stay = pltpu.make_async_copy(wo_ref, wo_dst, perm_recv)
-    pl.when(perm_away)(permute.start)
-    pl.when(jnp.logical_not(perm_away))(stay.start)
-
     shape = (4 * 16, 4 * 16)
     out_row, in_col = lax.broadcasted_iota(jnp.int32, shape, 0), lax.broadcasted_iota(jnp.int32, shape, 1)
     pick = ((out_row % 16) * KV + out_row // 16 == in_col).astype(jnp.float32).astype(jnp.bfloat16)
@@ -191,22 +180,16 @@
         sine[at, :] = jnp.where(lane < HD // 2, -wave, wave)
         return 0
 
+    lax.fori_loop(0, rows // 128, angles, 0)
     gain[...] = gain_ref[...].astype(jnp.float32).reshape(1, D)
 
-    def norm(i):
-        loads[i].wait()
-
-        def some(j, _):
-            at = pl.ds(pl.multiple_of(i * chunk + j * 16, 16), 16)
-            wide = hid[at, :].astype(jnp.float32)
-            meansq = jnp.sum(wide * wide, axis=1, keepdims=True) * (1.0 / D)
-            scaled = wide * lax.rsqrt(meansq + norm_eps)
-            for b in range(D // BLK):
-                cols = slice(b * BLK, (b + 1) * BLK)
-                x3[b, at, :] = (scaled[:, cols] * gain[:, cols]).astype(jnp.bfloat16)
-            return 0
-
-        lax.fori_loop(0, chunk // 16, some, 0)
+    line_peers = (lax.min(z + 1, 3) - z) + (z - lax.max(z - 1, 0))
+    pl.semaphore_wait(barrier, 10 + line_peers + perm_away.astype(jnp.int32) + (c + zh) % 2)
+
+    stream_q = Gather(wq_ref, full_q, recv_q, send_q, BLK // 2)
+    stream_s = Gather(full_s.at[rep], full_s, recv_s, send_s, full_s.shape[1] // 2)
+    stream_w = Gather(full_w.at[z], full_w, recv_w, send_w, 0, False)
+    stream_q.line(0)
 
     def piece(head, which):
         target = (head // 2) * 8 + (2 * (head % 2) + which) * 2 + zh
@@ -222,6 +205,32 @@
         pl.when(jnp.logical_not(away))(here.start)
         return made, away
 
+    pieces = [piece(head, which) for head in range(KV) for which in range(2)]
+
+    wo_dst = full_w.at[perm_dst[0] % 4]
+    permute = pltpu.make_async_remote_copy(
+        src_ref=wo_ref, dst_ref=wo_dst, send_sem=perm_send, recv_sem=perm_recv,
+        device_id=perm_dst, device_id_type=MESH,
+    )
+    stay = pltpu.make_async_copy(wo_ref, wo_dst, perm_recv)
+    pl.when(perm_away)(permute.start)
+    pl.when(jnp.logical_not(perm_away))(stay.start)
+
+    def norm(i):
+        loads[i].wait()
+
+        def some(j, _):
+            at = pl.ds(pl.multiple_of(i * chunk + j * 16, 16), 16)
+            wide = hid[at, :].astype(jnp.float32)
+            meansq = jnp.sum(wide * wide, axis=1, keepdims=True) * (1.0 / D)
+            scaled = wide * lax.rsqrt(meansq + norm_eps)
+            for b in range(D // BLK):
+                cols = slice(b * BLK, (b + 1) * BLK)
+                x3[b, at, :] = (scaled[:, cols] * gain[:, cols]).astype(jnp.bfloat16)
+            return 0
+
+        lax.fori_loop(0, chunk // 16, some, 0)
+
     def use_q(block, own=False):
         for i in range(rows // BLK):
             at = pl.ds(i * BLK, BLK)
@@ -238,25 +247,21 @@
             kacc[at, :] = part if own else kacc[at, :] + part
 
     norm(0)
-    pieces = [piece(head, which) for head in range(KV) for which in range(2)]
-    lax.fori_loop(0, rows // 128, angles, 0)
     norm(1)
     stream_q.line(1)
-    norm(2)
     for j in range(8):
         ref = full_s.at[rep, pl.ds(j * 16, 16)]
         pltpu.make_async_copy(ref, ref, kv_recv.at[j]).wait()
-    own_wo = full_s.at[rep, pl.ds(HD, BLK)]
-    pltpu.make_async_copy(own_wo, own_wo, perm_recv).wait()
     stream_s.line(0)
+    norm(2)
     norm(3)
+    stream_s.line(1)
+    norm(4)
     stream_q.line(2)
-    norm(4)
-    stream_s.line(1)
     norm(5)
+    stream_s.line(2)
+    norm(6)
     stream_q.line(3)
-    norm(6)
-    stream_s.line(2)
     norm(7)
     stream_s.line(3)
     own_load.wait()
@@ -265,6 +270,10 @@
     for k in range(4):
         lefts, rights = stream_q.ring(k, 0), stream_q.ring(k, 1)
         lefts_s, rights_s = stream_s.ring(k, 0), stream_s.ring(k, 1)
+        if k == 0:
+            own_wo = full_w.at[z]
+            pltpu.make_async_copy(own_wo, own_wo, perm_recv).wait()
+        stream_w.line(k)
         if k > 0:
             own_block = x * 4 + stream_q.order[k]
             use_q(own_block)
@@ -275,11 +284,10 @@
             use_s(block)
         if k > 0:
             use_q(stream_q.opposite(k - 1))
-    use_q(stream_q.opposite(3))
-    for k in range(4):
-        use_s(stream_s.opposite(k))
-    flush = pltpu.make_async_copy(full_s.at[:, pl.ds(HD, BLK)], wo_out, out_sem)
+            use_s(stream_s.opposite(k - 1))
+    flush = pltpu.make_async_copy(full_w, wo_out, out_sem)
     flush.start()
+    use_s(stream_s.opposite(3))
 
     fresh = kacc[...].astype(jnp.bfloat16).astype(jnp.float32)
     turned_key = fresh * cosine[...] + pltpu.roll(fresh, HD // 2, 1) * sine[...]
@@ -288,12 +296,12 @@
         src_ref=mine, dst_ref=other, send_sem=swap_sem.at[0], recv_sem=swap_sem.at[1],
         device_id=(rep, tp + 1 - 2 * c), device_id_type=MESH,
     )
+    use_q(stream_q.opposite(3))
+    swap.start()
     for h in range(q_ref.shape[1] // HD):
         cols = slice(h * HD, (h + 1) * HD)
         u = qacc[:, cols]
         q_ref[:, cols] = (u * cosine[...] + pltpu.roll(u, HD // 2, 1) * sine[...]).astype(jnp.bfloat16)
-        if h == 0:
-            swap.start()
     store_q = pltpu.make_async_copy(q_ref, q_out, store_sem.at[0])
     store_q.start()
     for made, away in pieces:
@@ -301,6 +309,7 @@
     pl.when(perm_away)(permute.wait_send)
     stream_q.drain()
     stream_s.drain()
+    stream_w.drain()
     swap.wait()
 
     @pl.when(c == 0)
@@ -344,7 +353,7 @@
             jax.ShapeDtypeStruct((rows, BLK), bf16),
             jax.ShapeDtypeStruct((rows, HD), bf16),
             jax.ShapeDtypeStruct((rows, HD), bf16),
-            jax.ShapeDtypeStruct((16, BLK, BLK), bf16),
+            jax.ShapeDtypeStruct((4, BLK, BLK), bf16),
         ),
         in_specs=[smem(), smem(), anywhere(), vmem(), vmem(), anywhere(), vmem(), anywhere()],
         out_specs=(anywhere(), anywhere(), anywhere(), anywhere()),
@@ -356,7 +365,8 @@
             pltpu.VMEM((rows, D), bf16),
             pltpu.VMEM((16, rows, BLK), bf16),
             pltpu.VMEM((16, BLK, BLK), bf16),
-            pltpu.VMEM((16, HD + BLK, BLK), bf16),
+            pltpu.VMEM((16, HD, BLK), bf16),
+            pltpu.VMEM((4, BLK, BLK), bf16),
             pltpu.VMEM((64, BLK), bf16),
             pltpu.VMEM((rows, BLK), f32),
             pltpu.VMEM((rows, HD), f32),
@@ -368,6 +378,8 @@
             dma((2, 16)),
             dma((24,)),
             dma((2, 16)),
+            dma((24,)),
+            dma((1, 4)),
             dma((24,)),
             dma((8,)),
             dma((8,)),
@@ -496,10 +508,10 @@
 
 
 def output_kernel(
-    att_ref, hidden_ref, gain_ref, wo_in,
-    resid_ref, normed_ref,
-    gain_row, wo_ref, att, part_send, part_recv, own, hid, sums_mine, sums,
-    hid_sem, ring_send, ring_recv, core_send, core_recv, part_sems, sum_send, sum_recv, wo_sem, own_sem,
+    att_ref, hidden_ref, wo_here,
+    resid_out, inverse_ref,
+    resid_ref, wo_ref, att, part_send, part_recv, own, hid, sums_mine, sums,
+    hid_sem, ring_send, ring_recv, core_send, core_recv, part_sems, sum_send, sum_recv, wo_sem, own_sem, wo_send, wo_recv, store_sem,
 ):
     rep, tp, x, z, zh, y, c = place()
     rows, width = hid.shape
@@ -507,15 +519,16 @@
         hidden_ref.at[:, pl.ds(pl.multiple_of(tp * width, width), width)], hid, hid_sem
     )
     load.start()
-    load_wo = pltpu.make_async_copy(wo_in, wo_ref, wo_sem)
+    load_wo = pltpu.make_async_copy(wo_here, wo_ref.at[pl.ds(x * 4, 4)], wo_sem)
     load_wo.start()
     load_own = pltpu.make_async_copy(att_ref, att.at[0, 0], own_sem)
     load_own.start()
-    gain_row[...] = gain_ref[...].astype(jnp.float32).reshape(1, D)
     barrier = pltpu.get_barrier_semaphore()
     for k in range(1, 16):
         signal(barrier, (rep, (tp + k) % 16))
-    pl.semaphore_wait(barrier, 15)
+    for dx in (1, 3):
+        signal(barrier, ((x + dx) % 4 * 4 + z, tp))
+    pl.semaphore_wait(barrier, 17)
 
     def at_y(to):
         return (rep, zh * 8 + (to % 4) * 2 + c)
@@ -561,39 +574,84 @@
         ref = att.at[0, 3, pl.ds(m * size, size)]
         send(ref, att.at[1, 3, pl.ds(m * size, size)], core_send.at[3, m], core_recv.at[3, m], partner)
 
-    def compute(m):
+    def columns(which):
+        return (1 - zh if which == 0 else zh) * 2
+
+    def beside(dx):
+        return ((x + dx) % 4 * 4 + z, tp)
+
+    def weight_out(which):
+        for side, dx in enumerate((1, 3)):
+            send(
+                wo_here.at[pl.ds(columns(which), 2)], wo_ref.at[pl.ds(x * 4 + columns(which), 2)],
+                wo_send.at[which, side], wo_recv.at[which, side], beside(dx),
+            )
+
+    def weight_relay(which):
+        for side, dx in enumerate((3, 1)):
+            at = pl.ds((x + dx) % 4 * 4 + columns(which), 2)
+            wait(wo_ref.at[at], wo_recv.at[which, side])
+            some = wo_ref.at[at, pl.ds(side * (BLK // 2), BLK // 2)]
+            send(some, some, wo_send.at[which, 2 + side], wo_recv.at[which, 2 + side], beside(4 - dx))
+
+    def weight_in(which):
+        for side in range(2):
+            some = pl.ds(side * (BLK // 2), BLK // 2)
+            wait(wo_ref.at[pl.ds((x + 2) % 4 * 4 + columns(which), 2), some], wo_recv.at[which, 2 + side])
+
+    def contract(at, target):
+        total = None
+        for side in range(2):
+            for d, dy in enumerate((0, 3, 1, 2)):
+                core = c if side == 0 else 1 - c
+                block = ((y + dy) % 4) * 4 + target * 2 + core
+                part = jnp.dot(att[side, d, at, :], wo_ref[block], preferred_element_type=jnp.float32)
+                total = part if total is None else total + part
+        return total
+
+    def away(m):
         at = pl.ds(m * size, size)
         for d in range(4):
             wait(att.at[1, d, at], core_recv.at[d, m])
-        for mine in range(2):
-            target = zh if mine else 1 - zh
-            total = None
-            for side in range(2):
-                for d, dy in enumerate((0, 3, 1, 2)):
-                    core = c if side == 0 else 1 - c
-                    block = ((y + dy) % 4) * 4 + target * 2 + core
-                    left = att[side, d, at, :]
-                    part = jnp.dot(left, wo_ref[block], preferred_element_type=jnp.float32)
-                    total = part if total is None else total + part
-            if mine:
-                own[at, :] = total
-            else:
-                part_send[at, :] = total.astype(jnp.bfloat16)
+        part_send[at, :] = contract(at, 1 - zh).astype(jnp.bfloat16)
         send(part_send.at[at], part_recv.at[at], part_sems.at[0, m], part_sems.at[1, m], across)
 
+    def mine(m):
+        at = pl.ds(m * BLK, BLK)
+        own[at, :] = contract(at, zh)
+
     own_send(0)
+    weight_out(0)
     own_send(1)
+    own_send(2)
     load_wo.wait()
     load_own.wait()
+    ready = 0
     for i in range(CHUNKS + 2):
         if i < CHUNKS:
             ring_in(i)
-        if i + 2 < CHUNKS:
-            own_send(i + 2)
+        if i + 3 < CHUNKS:
+            own_send(i + 3)
         if 1 <= i <= CHUNKS:
             far_in(i - 1)
-        if i >= 2:
-            compute(i - 2)
+        if i == 1:
+            weight_relay(0)
+            weight_out(1)
+        if i == WEIGHT_AT:
+            weight_in(0)
+        if i == CHUNKS - 2:
+            weight_relay(1)
+        if i >= WEIGHT_AT:
+            for _ in range(2):
+                if ready <= i - 2:
+                    away(ready)
+                    ready += 1
+        if i == CHUNKS:
+            weight_in(1)
+            for m in range(OWN_EARLY):
+                mine(m)
+    for m in range(OWN_EARLY, rows // BLK):
+        mine(m)
     load.wait()
     for m in range(CHUNKS):
         at = pl.ds(m * size, size)
@@ -608,36 +666,30 @@
             wide = resid.astype(jnp.float32)
             total = jnp.sum(wide * wide, axis=1, keepdims=True)
             sums_mine[pl.ds(row, 1), :] = jnp.transpose(jnp.broadcast_to(total, (HD, HD)))[:1, :]
+    store = pltpu.make_async_copy(resid_ref, resid_out, store_sem)
     for k in range(1, 16):
         send(sums_mine, sums.at[k], sum_send.at[k], sum_recv.at[k], (rep, (tp + k) % 16))
+    store.start()
     total = sums_mine[...]
     for k in range(1, 16):
         wait(sums.at[k], sum_recv.at[k])
         total = total + sums[k]
-    inverse = lax.rsqrt(total * (1.0 / D) + norm_eps)
-    gain = gain_row[:, pl.ds(pl.multiple_of(tp * width, width), width)]
-    for row in range(rows // HD):
-        here = pl.ds(row * HD, HD)
-        column = jnp.transpose(jnp.broadcast_to(inverse[row : row + 1, :], (HD, HD)))
-        for h in range(width // HD):
-            cols = slice(h * HD, (h + 1) * HD)
-            normed_ref[here, cols] = (
-                resid_ref[here, cols].astype(jnp.float32) * column * gain[:, cols]
-            ).astype(jnp.bfloat16)
+    inverse_ref[...] = lax.rsqrt(total * (1.0 / D) + norm_eps)
+    store.wait()
     for made in pending:
         made.wait_send()
 
 
-def finish(attended, hidden, out_gain, wo_blocks):
+def finish(attended, hidden, wo_here):
     rows, width = attended.shape
     bf16, f32, dma = jnp.bfloat16, jnp.float32, pltpu.SemaphoreType.DMA
     return pl.pallas_call(
         output_kernel,
-        out_shape=(jax.ShapeDtypeStruct((rows, width), bf16), jax.ShapeDtypeStruct((rows, width), bf16)),
-        in_specs=[anywhere(), anywhere(), vmem(), anywhere()],
-        out_specs=(vmem(), vmem()),
+        out_shape=(jax.ShapeDtypeStruct((rows, width), bf16), jax.ShapeDtypeStruct((rows // HD, HD), f32)),
+        in_specs=[anywhere(), anywhere(), anywhere()],
+        out_specs=(anywhere(), vmem()),
         scratch_shapes=[
-            pltpu.VMEM((1, D), f32),
+            pltpu.VMEM((rows, width), bf16),
             pltpu.VMEM((16, BLK, BLK), bf16),
             pltpu.VMEM((2, 4, rows, width), bf16),
             pltpu.VMEM((rows, width), bf16),
@@ -656,19 +708,75 @@
             dma((16,)),
             dma,
             dma,
+            dma((2, 4)),
+            dma((2, 4)),
+            dma,
         ],
         compiler_params=pltpu.CompilerParams(collective_id=1, has_side_effects=True, vmem_limit_bytes=VMEM_ALL),
         cost_estimate=pl.CostEstimate(flops=2 * 10**9, bytes_accessed=6 * 2**20, transcendentals=10**4),
         name="finish",
-    )(attended, hidden, out_gain, wo_blocks)
+    )(attended, hidden, wo_here)
+
+
+def scale_kernel(resid_in, inverse_ref, gain_ref, resid_out, normed_out, gain_row, resid, normed, in_sem, out_sem, norm_sem):
+    rows, width = resid.shape
+    count = in_sem.shape[0]
+    size = rows // count
+    loads, stores = [], []
+    for i in range(count):
+        at = pl.ds(i * size, size)
+        loads.append(pltpu.make_async_copy(resid_in.at[at], resid.at[at], in_sem.at[i]))
+        loads[-1].start()
+    gain_row[...] = gain_ref[...].astype(jnp.float32).reshape(1, D)
+    gain = gain_row[:, pl.ds(pl.multiple_of(lax.axis_index("tp") * width, width), width)]
+    for i in range(count):
+        at = pl.ds(i * size, size)
+        loads[i].wait()
+        stores.append(pltpu.make_async_copy(resid.at[at], resid_out.at[at], out_sem.at[i]))
+        stores[-1].start()
+        for row in range(i * size // HD, (i + 1) * size // HD):
+            here = pl.ds(row * HD, HD)
+            column = jnp.transpose(jnp.broadcast_to(inverse_ref[row : row + 1, :], (HD, HD)))
+            for h in range(width // HD):
+                cols = slice(h * HD, (h + 1) * HD)
+                normed[here, cols] = (
+                    resid[here, cols].astype(jnp.float32) * column * gain[:, cols]
+                ).astype(jnp.bfloat16)
+        stores.append(pltpu.make_async_copy(normed.at[at], normed_out.at[at], norm_sem.at[i]))
+        stores[-1].start()
+    for store in stores:
+        store.wait()
+
+
+def scale(resid, inverse, out_gain):
+    rows, width = resid.shape
+    bf16, dma = jnp.bfloat16, pltpu.SemaphoreType.DMA
+    return pl.pallas_call(
+        scale_kernel,
+        out_shape=(jax.ShapeDtypeStruct((rows, width), bf16), jax.ShapeDtypeStruct((rows, width), bf16)),
+        in_specs=[anywhere(), vmem(), vmem()],
+        out_specs=(anywhere(), anywhere()),
+        scratch_shapes=[
+            pltpu.VMEM((1, D), jnp.float32),
+            pltpu.VMEM((rows, width), bf16),
+            pltpu.VMEM((rows, width), bf16),
+            dma((4,)),
+            dma((4,)),
+            dma((4,)),
+        ],
+        compiler_params=pltpu.CompilerParams(vmem_limit_bytes=VMEM_ALL),
+        cost_estimate=pl.CostEstimate(flops=10**6, bytes_accessed=3 * 2**19, transcendentals=0),
+        name="scale",
+    )(resid, inverse, out_gain)
 
 
 def body(hidden, norm_gain, w_query, w_keyval, w_output, cache, lengths, prefix, out_gain):
     powers = np.arange(HD) % (HD // 2) * 2.0 / HD
     freqs = jnp.asarray((rope_base**-powers).astype(np.float32).reshape(1, HD))
-    q, k, v, wo_blocks = project(lengths, prefix, hidden, norm_gain, freqs, w_query, w_keyval.T, w_output)
+    q, k, v, wo_here = project(lengths, prefix, hidden, norm_gain, freqs, w_query, w_keyval.T, w_output)
     attended = attend(lengths, prefix, q, k, v, cache)
-    return finish(attended, hidden, out_gain, wo_blocks)
+    resid, inverse = finish(attended, hidden, wo_here)
+    return scale(resid, inverse, out_gain)
 
 
 def solution(mesh):

time: 140 us -> 123 us (0.88)
  Pallas kernels: 136 us -> 122 us
  local copies, waits for them, and re-layouts: 3.74 us -> 0 us
    pallas_call x1, Pallas kernels: 71.4 us -> 62.5 us  [project(): pl.pallas_call(project_kernel, out_shape=(jax.ShapeDtypeStruct((rows, BLK...]
    pallas_call x1, Pallas kernels: 54.8 us -> 48.5 us  [finish(): pl.pallas_call(output_kernel, out_shape=(jax.ShapeDtypeStruct((rows, widt...]
    unnamed x2 -> x0, local copies, waits for them, and re-layouts: 3.74 us -> none
    pallas_call x0 -> x1, Pallas kernels: none -> 2.79 us  [scale(): pl.pallas_call(scale_kernel, out_shape=(jax.ShapeDtypeStruct((rows, width...]
where the time goes in v4:
time: 123 us
  Pallas kernels  122 us (99%)
    pallas_call x1, Pallas kernels, project(): pl.pallas_call(project_kernel, out_shape=(jax.ShapeDtypeStruct((rows, BLK...  62.5 us
    pallas_call x1, Pallas kernels, finish(): pl.pallas_call(output_kernel, out_shape=(jax.ShapeDtypeStruct((rows, widt...  48.5 us
    pallas_call x1, Pallas kernels, attend(): pl.pallas_call(attention_kernel, out_shape=jax.ShapeDtypeStruct((rows, wi...  8.16 us
    pallas_call x1, Pallas kernels, scale(): pl.pallas_call(scale_kernel, out_shape=(jax.ShapeDtypeStruct((rows, width...  2.79 us

profile of v4, /device:TPU:1, one launch (start us, length us, event | category | flops | bytes accessed | tf_op | source)
XLA Modules:
  0.0 122.8 jit_solution(14504686784904081683)
XLA Ops:
  0.6 62.5 %project.1 = (bf16[1024,256]{1,0:T(8,128)(2,1)}, bf16[1024,128]{1,0:T(8,128)(2,1)}, bf16[1024,128]{1,0:T(8,128)(2,1)}, bf16[4,256,256]{2,1,0:T(8,128)(2,1)}) custom-call(s32[1,4]{1,0:T(1,128)} %lens_ref.3, s32[4]{0:T(128)} %pref_ref.3, bf16[1024,4096]{1,0:T(8,128)(2,1)} %hidden_ref.3, bf16[4096]{0:T(1024)(128)(2,1)} %gain_ref.2, ...), custom_call_target="tpu_custom_call" | custom-call | flops 3000000000 | bytes 12582912 | tf_op jit(solution)/shard_map/project/pallas_call | solution.py:350
  63.1 8.2 %attention.1.att_ref = bf16[1024,256]{1,0:T(8,128)(2,1)} custom-call(s32[1,4]{1,0:T(1,128)} %lens_ref.3, s32[4]{0:T(128)} %pref_ref.3, bf16[1024,256]{1,0:T(8,128)(2,1)} %get-tuple-element.8.q_ref, bf16[1024,128]{1,0:T(8,128)(2,1)} %get-tuple-element.9.k_ref, bf16[1024,128]{1,0:T(8,128)(2,1)} %get-tuple-element.10.v_ref, bf16[2048,1024]{1,0:T(8,128)(2,1)} %cache_ref.1), custom_call_target="tpu_custom_call" | custom-call | flops 2000000000 | bytes 3145728 | tf_op jit(solution)/shard_map/attention/pallas_call | solution.py:490
  71.3 48.5 %finish.1 = (bf16[1024,256]{1,0:T(8,128)(2,1)}, f32[8,128]{1,0:T(8,128)}) custom-call(bf16[1024,256]{1,0:T(8,128)(2,1)} %attention.1.att_ref, bf16[1024,4096]{1,0:T(8,128)(2,1)} %hidden_ref.3, bf16[4,256,256]{2,1,0:T(8,128)(2,1)} %get-tuple-element.11.wo_here), custom_call_target="tpu_custom_call" | custom-call | flops 2000000000 | bytes 6291456 | tf_op jit(solution)/shard_map/finish/pallas_call | solution.py:686
  119.8 2.8 %scale.1 = (bf16[1024,256]{1,0:T(8,128)(2,1)}, bf16[1024,256]{1,0:T(8,128)(2,1)}) custom-call(bf16[1024,256]{1,0:T(8,128)(2,1)} %get-tuple-element.12.resid_in, f32[8,128]{1,0:T(8,128)} %get-tuple-element.13.inverse_ref, bf16[4096]{0:T(1024)(128)(2,1)} %gain_ref.3), custom_call_target="tpu_custom_call" | custom-call | flops 1000000 | bytes 1572864 | tf_op jit(solution)/shard_map/scale/pallas_call | solution.py:754

commit v5 on v4

--- a/solution.py
+++ b/solution.py
@@ -124,7 +124,7 @@
     lens_ref, pref_ref, hidden_ref, gain_ref, freq_ref, wq_ref, wkv_ref, wo_ref,
     q_out, k_out, v_out, wo_out,
     gain, q_ref, k_ref, v_ref, hid, x3, full_q, full_s, full_w, turned, qacc, kacc, cosine, sine, mine, other,
-    hid_sem, recv_q, send_q, recv_s, send_s, recv_w, send_w, kv_send, kv_recv, perm_send, perm_recv, swap_sem, out_sem, own_sem, store_sem,
+    hid_sem, recv_q, send_q, recv_r, send_r, recv_s, send_s, recv_w, send_w, kv_send, kv_recv, perm_send, perm_recv, swap_sem, out_sem, own_sem, store_sem,
 ):
     rep, tp, x, z, zh, y, c = place()
     rows = hid.shape[0]
@@ -186,10 +186,13 @@
     line_peers = (lax.min(z + 1, 3) - z) + (z - lax.max(z - 1, 0))
     pl.semaphore_wait(barrier, 10 + line_peers + perm_away.astype(jnp.int32) + (c + zh) % 2)
 
-    stream_q = Gather(wq_ref, full_q, recv_q, send_q, BLK // 2)
+    low, high = pl.ds(0, BLK // 2), pl.ds(BLK // 2, BLK // 2)
+    stream_q = Gather(wq_ref.at[low], full_q.at[:, low], recv_q, send_q, BLK // 4)
+    stream_r = Gather(wq_ref.at[high], full_q.at[:, high], recv_r, send_r, BLK // 4)
     stream_s = Gather(full_s.at[rep], full_s, recv_s, send_s, full_s.shape[1] // 2)
     stream_w = Gather(full_w.at[z], full_w, recv_w, send_w, 0, False)
     stream_q.line(0)
+    stream_r.line(0)
 
     def piece(head, which):
         target = (head // 2) * 8 + (2 * (head % 2) + which) * 2 + zh
@@ -249,6 +252,7 @@
     norm(0)
     norm(1)
     stream_q.line(1)
+    stream_r.line(1)
     for j in range(8):
         ref = full_s.at[rep, pl.ds(j * 16, 16)]
         pltpu.make_async_copy(ref, ref, kv_recv.at[j]).wait()
@@ -257,23 +261,23 @@
     norm(3)
     stream_s.line(1)
     norm(4)
+    stream_s.line(2)
     stream_q.line(2)
+    stream_r.line(2)
     norm(5)
-    stream_s.line(2)
     norm(6)
+    stream_s.line(3)
     stream_q.line(3)
+    stream_r.line(3)
     norm(7)
-    stream_s.line(3)
     own_load.wait()
     use_q(rep, True)
     use_s(rep, True)
     for k in range(4):
+        lefts_s, rights_s = stream_s.ring(k, 0), stream_s.ring(k, 1)
         lefts, rights = stream_q.ring(k, 0), stream_q.ring(k, 1)
-        lefts_s, rights_s = stream_s.ring(k, 0), stream_s.ring(k, 1)
-        if k == 0:
-            own_wo = full_w.at[z]
-            pltpu.make_async_copy(own_wo, own_wo, perm_recv).wait()
-        stream_w.line(k)
+        stream_r.ring(k, 0)
+        stream_r.ring(k, 1)
         if k > 0:
             own_block = x * 4 + stream_q.order[k]
             use_q(own_block)
@@ -283,8 +287,13 @@
         for block in (lefts_s, rights_s):
             use_s(block)
         if k > 0:
+            stream_r.opposite(k - 1)
             use_q(stream_q.opposite(k - 1))
             use_s(stream_s.opposite(k - 1))
+        if k == 0:
+            own_wo = full_w.at[z]
+            pltpu.make_async_copy(own_wo, own_wo, perm_recv).wait()
+        stream_w.line(k)
     flush = pltpu.make_async_copy(full_w, wo_out, out_sem)
     flush.start()
     use_s(stream_s.opposite(3))
@@ -296,6 +305,7 @@
         src_ref=mine, dst_ref=other, send_sem=swap_sem.at[0], recv_sem=swap_sem.at[1],
         device_id=(rep, tp + 1 - 2 * c), device_id_type=MESH,
     )
+    stream_r.opposite(3)
     use_q(stream_q.opposite(3))
     swap.start()
     for h in range(q_ref.shape[1] // HD):
@@ -308,6 +318,7 @@
         pl.when(away)(made.wait_send)
     pl.when(perm_away)(permute.wait_send)
     stream_q.drain()
+    stream_r.drain()
     stream_s.drain()
     stream_w.drain()
     swap.wait()
@@ -375,6 +386,8 @@
             pltpu.VMEM((rows, HD), bf16),
             pltpu.VMEM((rows, HD), bf16),
             dma((8,)),
+            dma((2, 16)),
+            dma((24,)),
             dma((2, 16)),
             dma((24,)),
             dma((2, 16)),
@@ -636,10 +649,10 @@
             far_in(i - 1)
         if i == 1:
             weight_relay(0)
-            weight_out(1)
         if i == WEIGHT_AT:
             weight_in(0)
-        if i == CHUNKS - 2:
+            weight_out(1)
+        if i == CHUNKS - 1:
             weight_relay(1)
         if i >= WEIGHT_AT:
             for _ in range(2):

time: 123 us -> 124 us (level)
    pallas_call x1, Pallas kernels: 8.16 us -> 10.5 us  [attend(): pl.pallas_call(attention_kernel, out_shape=jax.ShapeDtypeStruct((rows, wi...]
    pallas_call x1, Pallas kernels: 48.5 us -> 47.3 us  [finish(): pl.pallas_call(output_kernel, out_shape=(jax.ShapeDtypeStruct((rows, widt...]
where the time goes in v5:
time: 124 us
  Pallas kernels  123 us (99%)
    pallas_call x1, Pallas kernels, project(): pl.pallas_call(project_kernel, out_shape=(jax.ShapeDtypeStruct((rows, BLK...  62.9 us
    pallas_call x1, Pallas kernels, finish(): pl.pallas_call(output_kernel, out_shape=(jax.ShapeDtypeStruct((rows, widt...  47.3 us
    pallas_call x1, Pallas kernels, attend(): pl.pallas_call(attention_kernel, out_shape=jax.ShapeDtypeStruct((rows, wi...  10.5 us
    pallas_call x1, Pallas kernels, scale(): pl.pallas_call(scale_kernel, out_shape=(jax.ShapeDtypeStruct((rows, width...  2.79 us

profile of v5, /device:TPU:1, one launch (start us, length us, event | category | flops | bytes accessed | tf_op | source)
XLA Modules:
  0.0 124.3 jit_solution(10887468798561581519)
XLA Ops:
  0.6 62.9 %project.1 = (bf16[1024,256]{1,0:T(8,128)(2,1)}, bf16[1024,128]{1,0:T(8,128)(2,1)}, bf16[1024,128]{1,0:T(8,128)(2,1)}, bf16[4,256,256]{2,1,0:T(8,128)(2,1)}) custom-call(s32[1,4]{1,0:T(1,128)} %lens_ref.3, s32[4]{0:T(128)} %pref_ref.3, bf16[1024,4096]{1,0:T(8,128)(2,1)} %hidden_ref.3, bf16[4096]{0:T(1024)(128)(2,1)} %gain_ref.2, ...), custom_call_target="tpu_custom_call" | custom-call | flops 3000000000 | bytes 12582912 | tf_op jit(solution)/shard_map/project/pallas_call | solution.py:361
  63.6 10.5 %attention.1.att_ref = bf16[1024,256]{1,0:T(8,128)(2,1)} custom-call(s32[1,4]{1,0:T(1,128)} %lens_ref.3, s32[4]{0:T(128)} %pref_ref.3, bf16[1024,256]{1,0:T(8,128)(2,1)} %get-tuple-element.8.q_ref, bf16[1024,128]{1,0:T(8,128)(2,1)} %get-tuple-element.9.k_ref, bf16[1024,128]{1,0:T(8,128)(2,1)} %get-tuple-element.10.v_ref, bf16[2048,1024]{1,0:T(8,128)(2,1)} %cache_ref.1), custom_call_target="tpu_custom_call" | custom-call | flops 2000000000 | bytes 3145728 | tf_op jit(solution)/shard_map/attention/pallas_call | solution.py:503
  74.0 47.3 %finish.1 = (bf16[1024,256]{1,0:T(8,128)(2,1)}, f32[8,128]{1,0:T(8,128)}) custom-call(bf16[1024,256]{1,0:T(8,128)(2,1)} %attention.1.att_ref, bf16[1024,4096]{1,0:T(8,128)(2,1)} %hidden_ref.3, bf16[4,256,256]{2,1,0:T(8,128)(2,1)} %get-tuple-element.11.wo_here), custom_call_target="tpu_custom_call" | custom-call | flops 2000000000 | bytes 6291456 | tf_op jit(solution)/shard_map/finish/pallas_call | solution.py:699
  121.3 2.8 %scale.1 = (bf16[1024,256]{1,0:T(8,128)(2,1)}, bf16[1024,256]{1,0:T(8,128)(2,1)}) custom-call(bf16[1024,256]{1,0:T(8,128)(2,1)} %get-tuple-element.12.resid_in, f32[8,128]{1,0:T(8,128)} %get-tuple-element.13.inverse_ref, bf16[4096]{0:T(1024)(128)(2,1)} %gain_ref.3), custom_call_target="tpu_custom_call" | custom-call | flops 1000000 | bytes 1572864 | tf_op jit(solution)/shard_map/scale/pallas_call | solution.py:767

commit v6 on v5

--- a/solution.py
+++ b/solution.py
@@ -180,7 +180,6 @@
         sine[at, :] = jnp.where(lane < HD // 2, -wave, wave)
         return 0
 
-    lax.fori_loop(0, rows // 128, angles, 0)
     gain[...] = gain_ref[...].astype(jnp.float32).reshape(1, D)
 
     line_peers = (lax.min(z + 1, 3) - z) + (z - lax.max(z - 1, 0))
@@ -250,6 +249,7 @@
             kacc[at, :] = part if own else kacc[at, :] + part
 
     norm(0)
+    lax.fori_loop(0, rows // 128, angles, 0)
     norm(1)
     stream_q.line(1)
     stream_r.line(1)

time: 124 us -> 123 us (level)
    pallas_call x1, Pallas kernels: 10.5 us -> 8.76 us  [attend(): pl.pallas_call(attention_kernel, out_shape=jax.ShapeDtypeStruct((rows, wi...]
where the time goes in v6:
time: 123 us
  Pallas kernels  122 us (99%)
    pallas_call x1, Pallas kernels, project(): pl.pallas_call(project_kernel, out_shape=(jax.ShapeDtypeStruct((rows, BLK...  62.8 us
    pallas_call x1, Pallas kernels, finish(): pl.pallas_call(output_kernel, out_shape=(jax.ShapeDtypeStruct((rows, widt...  47.6 us
    pallas_call x1, Pallas kernels, attend(): pl.pallas_call(attention_kernel, out_shape=jax.ShapeDtypeStruct((rows, wi...  8.76 us
    pallas_call x1, Pallas kernels, scale(): pl.pallas_call(scale_kernel, out_shape=(jax.ShapeDtypeStruct((rows, width...  2.79 us

profile of v6, /device:TPU:1, one launch (start us, length us, event | category | flops | bytes accessed | tf_op | source)
XLA Modules:
  0.0 122.7 jit_solution(343189345366603462)
XLA Ops:
  0.6 62.8 %project.1 = (bf16[1024,256]{1,0:T(8,128)(2,1)}, bf16[1024,128]{1,0:T(8,128)(2,1)}, bf16[1024,128]{1,0:T(8,128)(2,1)}, bf16[4,256,256]{2,1,0:T(8,128)(2,1)}) custom-call(s32[1,4]{1,0:T(1,128)} %lens_ref.3, s32[4]{0:T(128)} %pref_ref.3, bf16[1024,4096]{1,0:T(8,128)(2,1)} %hidden_ref.3, bf16[4096]{0:T(1024)(128)(2,1)} %gain_ref.2, ...), custom_call_target="tpu_custom_call" | custom-call | flops 3000000000 | bytes 12582912 | tf_op jit(solution)/shard_map/project/pallas_call | solution.py:361
  63.4 8.8 %attention.1.att_ref = bf16[1024,256]{1,0:T(8,128)(2,1)} custom-call(s32[1,4]{1,0:T(1,128)} %lens_ref.3, s32[4]{0:T(128)} %pref_ref.3, bf16[1024,256]{1,0:T(8,128)(2,1)} %get-tuple-element.8.q_ref, bf16[1024,128]{1,0:T(8,128)(2,1)} %get-tuple-element.9.k_ref, bf16[1024,128]{1,0:T(8,128)(2,1)} %get-tuple-element.10.v_ref, bf16[2048,1024]{1,0:T(8,128)(2,1)} %cache_ref.1), custom_call_target="tpu_custom_call" | custom-call | flops 2000000000 | bytes 3145728 | tf_op jit(solution)/shard_map/attention/pallas_call | solution.py:503
  72.2 47.6 %finish.1 = (bf16[1024,256]{1,0:T(8,128)(2,1)}, f32[8,128]{1,0:T(8,128)}) custom-call(bf16[1024,256]{1,0:T(8,128)(2,1)} %attention.1.att_ref, bf16[1024,4096]{1,0:T(8,128)(2,1)} %hidden_ref.3, bf16[4,256,256]{2,1,0:T(8,128)(2,1)} %get-tuple-element.11.wo_here), custom_call_target="tpu_custom_call" | custom-call | flops 2000000000 | bytes 6291456 | tf_op jit(solution)/shard_map/finish/pallas_call | solution.py:699
  119.8 2.8 %scale.1 = (bf16[1024,256]{1,0:T(8,128)(2,1)}, bf16[1024,256]{1,0:T(8,128)(2,1)}) custom-call(bf16[1024,256]{1,0:T(8,128)(2,1)} %get-tuple-element.12.resid_in, f32[8,128]{1,0:T(8,128)} %get-tuple-element.13.inverse_ref, bf16[4096]{0:T(1024)(128)(2,1)} %gain_ref.3), custom_call_target="tpu_custom_call" | custom-call | flops 1000000 | bytes 1572864 | tf_op jit(solution)/shard_map/scale/pallas_call | solution.py:767

commit v7 on v5

--- a/solution.py
+++ b/solution.py
@@ -528,6 +528,11 @@
 ):
     rep, tp, x, z, zh, y, c = place()
     rows, width = hid.shape
+    barrier = pltpu.get_barrier_semaphore()
+    for k in sorted(range(1, 16), key=lambda k: abs(k - 8)):
+        signal(barrier, (rep, (tp + k) % 16))
+    for dx in (1, 3):
+        signal(barrier, ((x + dx) % 4 * 4 + z, tp))
     load = pltpu.make_async_copy(
         hidden_ref.at[:, pl.ds(pl.multiple_of(tp * width, width), width)], hid, hid_sem
     )
@@ -536,11 +541,6 @@
     load_wo.start()
     load_own = pltpu.make_async_copy(att_ref, att.at[0, 0], own_sem)
     load_own.start()
-    barrier = pltpu.get_barrier_semaphore()
-    for k in range(1, 16):
-        signal(barrier, (rep, (tp + k) % 16))
-    for dx in (1, 3):
-        signal(barrier, ((x + dx) % 4 * 4 + z, tp))
     pl.semaphore_wait(barrier, 17)
 
     def at_y(to):
@@ -680,7 +680,7 @@
             total = jnp.sum(wide * wide, axis=1, keepdims=True)
             sums_mine[pl.ds(row, 1), :] = jnp.transpose(jnp.broadcast_to(total, (HD, HD)))[:1, :]
     store = pltpu.make_async_copy(resid_ref, resid_out, store_sem)
-    for k in range(1, 16):
+    for k in sorted(range(1, 16), key=lambda k: abs(k - 8)):
         send(sums_mine, sums.at[k], sum_send.at[k], sum_recv.at[k], (rep, (tp + k) % 16))
     store.start()
     total = sums_mine[...]

time: 124 us -> 123 us (level)
    pallas_call x1, Pallas kernels: 10.5 us -> 8.76 us  [attend(): pl.pallas_call(attention_kernel, out_shape=jax.ShapeDtypeStruct((rows, wi...]
where the time goes in v7:
time: 123 us
  Pallas kernels  122 us (99%)
    pallas_call x1, Pallas kernels, project(): pl.pallas_call(project_kernel, out_shape=(jax.ShapeDtypeStruct((rows, BLK...  62.9 us
    pallas_call x1, Pallas kernels, finish(): pl.pallas_call(output_kernel, out_shape=(jax.ShapeDtypeStruct((rows, widt...  47.7 us
    pallas_call x1, Pallas kernels, attend(): pl.pallas_call(attention_kernel, out_shape=jax.ShapeDtypeStruct((rows, wi...  8.76 us
    pallas_call x1, Pallas kernels, scale(): pl.pallas_call(scale_kernel, out_shape=(jax.ShapeDtypeStruct((rows, width...  2.79 us

profile of v7, /device:TPU:1, one launch (start us, length us, event | category | flops | bytes accessed | tf_op | source)
XLA Modules:
  0.0 122.9 jit_solution(4523743208980205323)
XLA Ops:
  0.6 62.9 %project.1 = (bf16[1024,256]{1,0:T(8,128)(2,1)}, bf16[1024,128]{1,0:T(8,128)(2,1)}, bf16[1024,128]{1,0:T(8,128)(2,1)}, bf16[4,256,256]{2,1,0:T(8,128)(2,1)}) custom-call(s32[1,4]{1,0:T(1,128)} %lens_ref.3, s32[4]{0:T(128)} %pref_ref.3, bf16[1024,4096]{1,0:T(8,128)(2,1)} %hidden_ref.3, bf16[4096]{0:T(1024)(128)(2,1)} %gain_ref.2, ...), custom_call_target="tpu_custom_call" | custom-call | flops 3000000000 | bytes 12582912 | tf_op jit(solution)/shard_map/project/pallas_call | solution.py:361
  63.6 8.8 %attention.1.att_ref = bf16[1024,256]{1,0:T(8,128)(2,1)} custom-call(s32[1,4]{1,0:T(1,128)} %lens_ref.3, s32[4]{0:T(128)} %pref_ref.3, bf16[1024,256]{1,0:T(8,128)(2,1)} %get-tuple-element.8.q_ref, bf16[1024,128]{1,0:T(8,128)(2,1)} %get-tuple-element.9.k_ref, bf16[1024,128]{1,0:T(8,128)(2,1)} %get-tuple-element.10.v_ref, bf16[2048,1024]{1,0:T(8,128)(2,1)} %cache_ref.1), custom_call_target="tpu_custom_call" | custom-call | flops 2000000000 | bytes 3145728 | tf_op jit(solution)/shard_map/attention/pallas_call | solution.py:503
  72.3 47.7 %finish.1 = (bf16[1024,256]{1,0:T(8,128)(2,1)}, f32[8,128]{1,0:T(8,128)}) custom-call(bf16[1024,256]{1,0:T(8,128)(2,1)} %attention.1.att_ref, bf16[1024,4096]{1,0:T(8,128)(2,1)} %hidden_ref.3, bf16[4,256,256]{2,1,0:T(8,128)(2,1)} %get-tuple-element.11.wo_here), custom_call_target="tpu_custom_call" | custom-call | flops 2000000000 | bytes 6291456 | tf_op jit(solution)/shard_map/finish/pallas_call | solution.py:699
  120.0 2.8 %scale.1 = (bf16[1024,256]{1,0:T(8,128)(2,1)}, bf16[1024,256]{1,0:T(8,128)(2,1)}) custom-call(bf16[1024,256]{1,0:T(8,128)(2,1)} %get-tuple-element.12.resid_in, f32[8,128]{1,0:T(8,128)} %get-tuple-element.13.inverse_ref, bf16[4096]{0:T(1024)(128)(2,1)} %gain_ref.3), custom_call_target="tpu_custom_call" | custom-call | flops 1000000 | bytes 1572864 | tf_op jit(solution)/shard_map/scale/pallas_call | solution.py:767

commit v8 on v5

--- a/solution.py
+++ b/solution.py
@@ -773,9 +773,9 @@
             pltpu.VMEM((1, D), jnp.float32),
             pltpu.VMEM((rows, width), bf16),
             pltpu.VMEM((rows, width), bf16),
-            dma((4,)),
-            dma((4,)),
-            dma((4,)),
+            dma((8,)),
+            dma((8,)),
+            dma((8,)),
         ],
         compiler_params=pltpu.CompilerParams(vmem_limit_bytes=VMEM_ALL),
         cost_estimate=pl.CostEstimate(flops=10**6, bytes_accessed=3 * 2**19, transcendentals=0),

time: 124 us -> 125 us (level); the launches traced: 124 us -> 124 us
    pallas_call x1, Pallas kernels: 10.5 us -> 8.45 us  [attend(): pl.pallas_call(attention_kernel, out_shape=jax.ShapeDtypeStruct((rows, wi...]
where the time goes in v8:
time: 125 us; the launch traced here: 124 us
  Pallas kernels  123 us (98%)
    pallas_call x1, Pallas kernels, project(): pl.pallas_call(project_kernel, out_shape=(jax.ShapeDtypeStruct((rows, BLK...  62.9 us
    pallas_call x1, Pallas kernels, finish(): pl.pallas_call(output_kernel, out_shape=(jax.ShapeDtypeStruct((rows, widt...  48.4 us
    pallas_call x1, Pallas kernels, attend(): pl.pallas_call(attention_kernel, out_shape=jax.ShapeDtypeStruct((rows, wi...  8.45 us
    pallas_call x1, Pallas kernels, scale(): pl.pallas_call(scale_kernel, out_shape=(jax.ShapeDtypeStruct((rows, width...  3.22 us

profile of v8, /device:TPU:1, one launch (start us, length us, event | category | flops | bytes accessed | tf_op | source)
XLA Modules:
  0.0 123.8 jit_solution(3622869854450880547)
XLA Ops:
  0.6 62.9 %project.1 = (bf16[1024,256]{1,0:T(8,128)(2,1)}, bf16[1024,128]{1,0:T(8,128)(2,1)}, bf16[1024,128]{1,0:T(8,128)(2,1)}, bf16[4,256,256]{2,1,0:T(8,128)(2,1)}) custom-call(s32[1,4]{1,0:T(1,128)} %lens_ref.3, s32[4]{0:T(128)} %pref_ref.3, bf16[1024,4096]{1,0:T(8,128)(2,1)} %hidden_ref.3, bf16[4096]{0:T(1024)(128)(2,1)} %gain_ref.2, ...), custom_call_target="tpu_custom_call" | custom-call | flops 3000000000 | bytes 12582912 | tf_op jit(solution)/shard_map/project/pallas_call | solution.py:361
  63.6 8.5 %attention.1.att_ref = bf16[1024,256]{1,0:T(8,128)(2,1)} custom-call(s32[1,4]{1,0:T(1,128)} %lens_ref.3, s32[4]{0:T(128)} %pref_ref.3, bf16[1024,256]{1,0:T(8,128)(2,1)} %get-tuple-element.8.q_ref, bf16[1024,128]{1,0:T(8,128)(2,1)} %get-tuple-element.9.k_ref, bf16[1024,128]{1,0:T(8,128)(2,1)} %get-tuple-element.10.v_ref, bf16[2048,1024]{1,0:T(8,128)(2,1)} %cache_ref.1), custom_call_target="tpu_custom_call" | custom-call | flops 2000000000 | bytes 3145728 | tf_op jit(solution)/shard_map/attention/pallas_call | solution.py:503
  72.0 48.4 %finish.1 = (bf16[1024,256]{1,0:T(8,128)(2,1)}, f32[8,128]{1,0:T(8,128)}) custom-call(bf16[1024,256]{1,0:T(8,128)(2,1)} %attention.1.att_ref, bf16[1024,4096]{1,0:T(8,128)(2,1)} %hidden_ref.3, bf16[4,256,256]{2,1,0:T(8,128)(2,1)} %get-tuple-element.11.wo_here), custom_call_target="tpu_custom_call" | custom-call | flops 2000000000 | bytes 6291456 | tf_op jit(solution)/shard_map/finish/pallas_call | solution.py:699
  120.4 3.2 %scale.1 = (bf16[1024,256]{1,0:T(8,128)(2,1)}, bf16[1024,256]{1,0:T(8,128)(2,1)}) custom-call(bf16[1024,256]{1,0:T(8,128)(2,1)} %get-tuple-element.12.resid_in, f32[8,128]{1,0:T(8,128)} %get-tuple-element.13.inverse_ref, bf16[4096]{0:T(1024)(128)(2,1)} %gain_ref.3), custom_call_target="tpu_custom_call" | custom-call | flops 1000000 | bytes 1572864 | tf_op jit(solution)/shard_map/scale/pallas_call | solution.py:767
